TPU v7x, 256 devices: a whole 4x4x8 slice. The times are simulated.
256 devices in a mesh: req: 32 (over x, y, core), exp: 8 (over z).
Axes of the slice: x: 4, y: 4, z: 8, core: 2. Of those that a mesh axis runs over, the one named last changes fastest.
Arguments:
- residual: bfloat16 [4096, 2048], P(('req', 'exp')), may hold values from -12 to 12
- queries: bfloat16 [4096, 2, 2048], P('req', None, 'exp'), may hold values from -9 to 9
- kv_cache: bfloat16 [608, 2, 128, 2048], P('req', None, None, 'exp'), may hold values from -4 to 4
- page_table: int32 [288, 11], P('req'), may hold values from 0 to 18, as said below
- seq_lengths: int32 [288], P('req'), may hold values from 8 to 1408, as said below
- head_route: int32 [4096, 2], P('req'), may hold values from 0 to 7, all different within a row
- head_gate: float32 [4096, 2], P('req'), may hold values from 0.2 to 1
- out_weight: bfloat16 [8, 2048, 2048], P(None, 'exp'), may hold values from -0.5 to 0.5
- norm_gain: float32 [2048], replicated, may hold values from 0.25 to 1.75
- expert_route: int32 [4096, 2], P(('req', 'exp')), may hold values from 0 to 7, all different within a row; in each aligned block of 16 rows (0 to 15, 16 to 31, ...) at most 8 rows name the same one
- expert_gate: float32 [4096, 2], P(('req', 'exp')), may hold values from 0.2 to 1
- gate_up: bfloat16 [8, 2, 2048, 5632], P('exp', None, None, 'req'), may hold values from -0.125 to 0.125
- down_weight: bfloat16 [8, 5632, 2048], P('exp', 'req'), may hold values from -0.078125 to 0.078125
Outputs:
- attended: bfloat16 [4096, 2048], P(('req', 'exp'))
- expert_mix: bfloat16 [4096, 2048], P(('req', 'exp'))
Inputs may be any that keep to these rules, and one draw needn't show every extreme that they name: `page_table`: pages are numbered within the slot's group. A group's slot 0 lists 11 different pages; each other slot repeats one page along its row; no two slots of a group share a page. `seq_lengths`: slot 0 of every group is a prefill request of length at least 120; the other slots are decode requests of length at most 128. `head_route`: each row names 2 different attention experts. `expert_route`: each row names 2 different experts; within the rows of one device no expert is named by more than 8 rows.
All inputs are finite; a program needn't handle non-finite values.
Results may differ from a plain program's by a relative error of at most 0.023.
Values may be sent and summed in bfloat16 or wider, within the bound.
A program may use at most 128 MiB of HBM per device.

v0:
```python
import jax
import jax.numpy as jnp
from jax import lax
from jax.sharding import PartitionSpec as P

HD = 128
TOPA = 2
SPAN = 120


def attend_local(queries_one, key_rows, value_rows, positions, head_count):
    amount = queries_one.shape[0]
    heads_q = queries_one.reshape(amount * TOPA, head_count, HD)
    heads_k = key_rows.reshape(-1, head_count, HD)
    heads_v = value_rows.reshape(-1, head_count, HD)
    scores = jnp.einsum(
        "qhd,khd->hqk", heads_q, heads_k, preferred_element_type=jnp.float32
    ) * HD ** (-0.5)
    key_pos = jnp.arange(heads_k.shape[0], dtype=jnp.int32)
    row_pos = jnp.repeat(positions, TOPA)
    allowed = key_pos[None, :] <= row_pos[:, None]
    scores = jnp.where(allowed[None], scores, -1e30)
    row_max = jnp.max(scores, axis=2, keepdims=True)
    raised = jnp.exp(scores - row_max)
    attention_weights = (raised / jnp.sum(raised, axis=2, keepdims=True)).astype(jnp.bfloat16)
    mixture = jnp.einsum(
        "hqk,khd->qhd", attention_weights, heads_v, preferred_element_type=jnp.float32
    )
    return mixture.astype(jnp.bfloat16).reshape(amount, TOPA, head_count * HD)


def local(
    residual,
    queries,
    kv_cache,
    page_table,
    seq_lengths,
    head_route,
    head_gate,
    out_weight,
    norm_gain,
    expert_route,
    expert_gate,
    gate_up,
    down_weight,
):
    feature_width = queries.shape[2]
    head_count = feature_width // HD
    page_rows = kv_cache[page_table[0]]
    key_rows = page_rows[:, 0].reshape(-1, feature_width)
    value_rows = page_rows[:, 1].reshape(-1, feature_width)
    prefill_pos = seq_lengths[0] - SPAN + jnp.arange(SPAN, dtype=jnp.int32)
    prefill_out = attend_local(queries[:SPAN], key_rows, value_rows, prefill_pos, head_count)
    decode_pages = kv_cache[page_table[1:, 0]]

    def decode_one(query_row, page_block, length):
        return attend_local(
            query_row[None], page_block[0], page_block[1], (length - 1)[None], head_count
        )[0]

    decode_out = jax.vmap(decode_one)(queries[SPAN:], decode_pages, seq_lengths[1:])
    mixture = jnp.concatenate([prefill_out, decode_out], axis=0)
    partial_value = jnp.zeros((mixture.shape[0], residual.shape[1]), jnp.float32)
    for expert_index in range(out_weight.shape[0]):
        picked = head_route == expert_index
        chosen = jnp.sum(jnp.where(picked[:, :, None], mixture, jnp.zeros_like(mixture)), axis=1)
        weight = jnp.sum(jnp.where(picked, head_gate, jnp.zeros_like(head_gate)), axis=1)
        partial_value = partial_value + weight[:, None] * jnp.dot(
            chosen, out_weight[expert_index], preferred_element_type=jnp.float32
        )
    row_count = residual.shape[0]
    summed = lax.psum(partial_value.astype(jnp.bfloat16), "exp").astype(jnp.float32)
    own_heads = lax.dynamic_slice_in_dim(summed, lax.axis_index("exp") * row_count, row_count, 0)
    attended = (residual.astype(jnp.float32) + own_heads).astype(jnp.bfloat16)
    values_f = attended.astype(jnp.float32)
    normed = (
        values_f
        * lax.rsqrt(jnp.mean(values_f * values_f, axis=1, keepdims=True) + 1e-06)
        * norm_gain
    ).astype(jnp.bfloat16)
    experts = lax.axis_size("exp")
    capacity = max(2, 2 * TOPA * row_count // experts)
    flat_route = expert_route.reshape(-1)
    onehot = (flat_route[:, None] == jnp.arange(experts, dtype=jnp.int32)[None, :]).astype(
        jnp.int32
    )
    earlier = jnp.cumsum(onehot, axis=0) - onehot
    rank_index = jnp.sum(earlier * onehot, axis=1)
    slot_index = flat_route * capacity + rank_index
    placing = (
        jnp.arange(experts * capacity, dtype=jnp.int32)[:, None] == slot_index[None, :]
    ).astype(jnp.bfloat16)
    repeated = jnp.repeat(normed, TOPA, axis=0)
    outgoing = jnp.dot(placing, repeated, preferred_element_type=jnp.float32).astype(jnp.bfloat16)
    w_gate = gate_up[0, 0]
    w_up = gate_up[0, 1]
    w_down = down_weight[0]
    arrived = lax.all_to_all(outgoing, "exp", split_axis=0, concat_axis=0, tiled=True)
    portion = lax.all_gather(arrived, "req", axis=0, tiled=True)
    gate_part = jnp.dot(portion, w_gate, preferred_element_type=jnp.float32)
    up_part = jnp.dot(portion, w_up, preferred_element_type=jnp.float32)
    active = (jax.nn.silu(gate_part) * up_part).astype(jnp.bfloat16)
    portion = active
    returned = lax.psum_scatter(
        jnp.dot(portion, w_down, preferred_element_type=jnp.float32).astype(jnp.bfloat16),
        "req",
        scatter_dimension=0,
        tiled=True,
    )
    homeward = lax.all_to_all(returned, "exp", split_axis=0, concat_axis=0, tiled=True)
    picked_rows = jnp.take(homeward, slot_index, axis=0).astype(jnp.float32)
    weighted = picked_rows * expert_gate.reshape(-1)[:, None]
    expert_mix = jnp.sum(weighted.reshape(row_count, TOPA, -1), axis=1).astype(jnp.bfloat16)
    return (attended, expert_mix)


def solution(mesh):
    return jax.shard_map(
        local,
        mesh=mesh,
        in_specs=(
            P(("req", "exp"), None),
            P("req", None, "exp"),
            P("req", None, None, "exp"),
            P("req", None),
            P("req"),
            P("req", None),
            P("req", None),
            P(None, "exp", None),
            P(),
            P(("req", "exp"), None),
            P(("req", "exp"), None),
            P("exp", None, None, "req"),
            P("exp", "req", None),
        ),
        out_specs=(P(("req", "exp"), None), P(("req", "exp"), None)),
        check_vma=False,
    )
```

profile of v0, /device:TPU:2, one launch (start us, length us, event | category | flops | bytes accessed | tf_op | source)
XLA Modules:
  0.0 351.9 jit_solution(16315062266536121598)
XLA Ops:
  7.2 0.8 fusion.78
  8.1 0.8 fusion.77
  8.9 1.3 select_reduce_fusion.1
  10.2 0.1 copy.62
  10.3 0.7 copy.71
  11.1 0.7 copy.72
  11.8 0.7 copy.73
  12.5 0.7 copy.74
  13.2 0.7 copy.75
  13.9 0.7 copy.76
  14.7 0.7 copy.77
  15.4 1.8 gather_fusion
  17.2 2.4 fusion.83
  19.6 2.6 reshape_reshape_squeeze.7
  22.2 0.6 slice_add_fusion
  22.9 0.1 le.49
  23.0 1.0 iota_compare_fusion
  24.0 0.1 reshape.164
  24.1 1.1 reshape_reshape_squeeze.6
  25.2 3.9 %fusion.86 = (f32[2,240]{1,0:T(2,128)S(1)}, f32[2,240,1408]{2,1,0:T(8,128)}) fusion(pred[240,1408]{1,0:T(8,128)(4,1)} %iota_compare_fusion, bf16[1408,2,128]{2,1,0:T(2,128)(2,1)} %reshape_reshape_squeeze.7, bf16[240,2,128]{2,1,0:T(2,128)(2,1)S(1)} %reshape.164), kind=kOutput, calls=%fused_computation.145 | convolution fusion | flops 175719808 | bytes 3886976 | tf_op jit(solution)/shard_map/sub | solution.py:24
  29.0 2.4 fusion.18
  31.4 0.1 copy.66
  31.5 0.7 reshape.165
  32.2 0.6 pad_clamp_fusion.1
  32.8 0.7 gather_fusion.1
  33.6 1.1 fusion.84
  34.6 1.3 copy.68
  36.0 1.3 iota_compare_fusion.4
  37.2 1.3 copy.67
  38.5 2.2 fusion.85
  40.8 1.1 fusion.23
  41.9 3.8 %fusion.63 = (bf16[128,256]{1,0:T(8,128)(2,1)S(1)}, bf16[128,256]{1,0:T(8,128)(2,1)S(1)}, bf16[128,256]{1,0:T(8,128)(2,1)S(1)}, bf16[128,256]{1,0:T(8,128)(2,1)S...) fusion(pred[128,2]{1,0:T(8,128)(4,1)} %copy.77, ...), kind=kLoop, calls=%fused_computation.90 | loop fusion | flops 851968 | bytes 657408 | tf_op jit(solution)/shard_map/reduce_sum | solution.py:66
  45.7 1.5 convolution_multiply_fusion.9
  47.3 1.5 fusion.13
  48.9 1.5 fusion.12
  50.4 1.5 fusion.11
  52.0 1.5 fusion.10
  53.6 1.5 fusion.9
  55.2 1.6 fusion.8
  56.7 2.4 fusion.14
  59.2 0.1 copy.78
  59.3 0.1 reshape.167
  59.5 0.2 select_reduce_fusion
  59.7 76.3 %all-reduce.2.cloned.1.call-done = bf16[128,2048]{1,0:T(8,128)(2,1)} async-done(((bf16[128,2048]{1,0:T(8,128)(2,1)}), bf16[128,2048]{1,0:T(8,128)(2,1)}) %all-reduce.2.cloned.1.call-update) | async-done | bytes 524304 | tf_op jit(solution)/shard_map/psum | solution.py:72
  136.0 1.0 fusion.53
  137.0 0.1 fusion.55
  137.2 0.2 fusion.15
  137.4 14.4 %all_to_all.24 = bf16[8,8,2048]{2,1,0:T(8,128)(2,1)} all-to-all(bf16[8,8,2048]{2,1,0:T(8,128)(2,1)S(1)} %fusion.15), channel_id=1, replica_groups=mesh['req'=32,'exp'=8] {'exp'}, dimensions={0} | all-to-all | bytes 524288 | tf_op jit(solution)/shard_map/all_to_all | solution.py:98
  151.9 0.2 reduce-scatter.2.cloned.1.call-start
  152.1 53.8 %all-gather.2.cloned.1.call-done = bf16[2048,2048]{1,0:T(8,128)(2,1)} async-done(((bf16[64,2048]{1,0:T(8,128)(2,1)}), bf16[2048,2048]{1,0:T(8,128)(2,1)}) %all-gather.2.cloned.1.call-update) | async-done | bytes 8388624 | tf_op jit(solution)/shard_map/all_gather | solution.py:99
  205.9 7.5 %fusion.43 = f32[2048,176]{0,1:T(8,128)} fusion(bf16[2048,2048]{1,0:T(8,128)(2,1)} %all-gather.2.cloned.1.call-done, bf16[1,2,2048,176]{2,3,1,0:T(8,128)(2,1)} %param.24), kind=kOutput, calls=%fused_computation.61 | convolution fusion | flops 1476395008 | bytes 10551296 | tf_op jit(solution)/shard_map/dot_general | solution.py:100
  213.5 12.5 %convolution_convert_fusion = bf16[2048,2048]{1,0:T(8,128)(2,1)} fusion(bf16[2048,2048]{1,0:T(8,128)(2,1)} %all-gather.2.cloned.1.call-done, f32[2048,176]{0,1:T(8,128)} %fusion.43, bf16[1,176,2048]{2,1,0:T(8,128)(2,1)} %param.25, bf16[1,2,2048,176]{2,3,1,0:T(8,128)(2,1)} %param.24), kind=kOutput, calls=%fused_computation.5 | convolution fusion | flops 2959147008 | bytes 19660800 | tf_op jit(solution)/shard_map/dot_general | solution.py:105
  226.0 0.1 reduce_sum.236
  226.1 0.1 copy.81
  226.2 0.1 mul.185
  226.3 0.1 copy.79
  226.4 99.6 %reduce-scatter.2.cloned.1.call-done = bf16[64,2048]{1,0:T(8,128)(2,1)} async-done(((bf16[2048,2048]{1,0:T(8,128)(2,1)}), bf16[64,2048]{1,0:T(8,128)(2,1)}) %reduce-scatter.2.cloned.1.call-update) | async-done | bytes 262160 | tf_op jit(solution)/shard_map/reduce_scatter | solution.py:104
  326.0 7.0 %all-to-all-start.1 = ((bf16[8,8,2048]{2,1,0:T(8,128)(2,1)}), bf16[8,8,2048]{2,1,0:T(8,128)(2,1)S(1)}, u32[]{:S(2)}, u32[]{:S(2)}) async-start(bf16[8,8,2048]{2,1,0:T(8,128)(2,1)} %bitcast.101), calls=%async_computation.2 | async-start | bytes 524288 | tf_op jit(solution)/shard_map/all_to_all | solution.py:110
  333.0 0.1 copy.80
  333.1 0.1 copy.82
  333.2 10.3 %all-to-all-done.1 = bf16[8,8,2048]{2,1,0:T(8,128)(2,1)S(1)} async-done(((bf16[8,8,2048]{2,1,0:T(8,128)(2,1)}), bf16[8,8,2048]{2,1,0:T(8,128)(2,1)S(1)}, u32[]{:S(2)}, u32[]{:S(2)}) %all-to-all-start.1) | async-done | bytes 262176 | tf_op jit(solution)/shard_map/all_to_all | solution.py:110
  343.4 0.6 gather_fusion.2
  344.1 0.1 gather.15
  344.2 1.2 multiply_reduce_fusion
  (50 shorter events, 0.6 us)
Async XLA Ops:
  7.2 8.2 %copy-start = (bf16[19,2,128,256]{3,2,1,0:T(8,128)(2,1)S(1)}, bf16[19,2,128,256]{3,2,1,0:T(8,128)(2,1)}, u32[]{:S(2)}) copy-start(bf16[19,2,128,256]{3,2,1,0:T(8,128)(2,1)} %param.15) | copy-start | bytes 7471108
  7.2 128.8 %all-reduce.2.cloned.1.call-start = ((), (), s32[]{:S(2)}) async-start(), calls=%async_computation.3 | async-start | bytes 1048576 | tf_op jit(solution)/shard_map/psum | solution.py:72
  17.2 5.0 %copy-start.14 = (s32[9]{0:T(128)S(1)}, s32[9]{0:T(128)}, u32[]{:S(2)}) copy-start(s32[9]{0:T(128)} %param.17) | copy-start | bytes 112
  17.2 6.8 %slice-start = ((bf16[128,2,256]{2,1,0:T(2,128)(2,1)}), bf16[120,2,256]{2,1,0:T(2,128)(2,1)S(1)}, s32[]{:S(2)}) async-start(bf16[128,2,256]{2,1,0:T(2,128)(2,1)} %param.14), calls=%async_computation.6 | async-start | bytes 245760 | tf_op jit(solution)/shard_map/slice | solution.py:53
  25.2 3.9 %copy-start.1 = (bf16[1408,2,128]{2,1,0:T(2,128)(2,1)S(1)}, bf16[1408,2,128]{2,1,0:T(2,128)(2,1)}, u32[]{:S(2)}) copy-start(bf16[1408,2,128]{2,1,0:T(2,128)(2,1)} %reshape_reshape_squeeze.6) | copy-start | bytes 2162692
  40.8 6.5 %copy-start.12 = (f32[128]{0:T(128)S(1)}, f32[128]{0:T(128)}, u32[]{:S(2)}) copy-start(f32[128]{0:T(128)} %get-tuple-element.15) | copy-start | bytes 1540
  45.7 3.1 copy-start.11
  47.3 3.1 copy-start.10
  48.9 3.1 copy-start.9
  50.4 3.1 copy-start.8
  52.0 3.1 copy-start.7
  53.6 3.2 copy-start.6
  55.1 4.1 %copy-start.4 = (s32[16,2]{0,1:T(2,128)S(1)}, s32[16,2]{0,1:T(2,128)}, u32[]{:S(2)}) copy-start(s32[16,2]{0,1:T(2,128)} %param.22) | copy-start | bytes 388
  55.1 80.8 %copy-start.3 = (bf16[16,2048]{1,0:T(8,128)(2,1)S(1)}, bf16[16,2048]{1,0:T(8,128)(2,1)}, u32[]{:S(2)}) copy-start(bf16[16,2048]{1,0:T(8,128)(2,1)} %param.13) | copy-start | bytes 196612
  55.1 81.8 %copy-start.5 = (f32[2048]{0:T(1024)S(1)}, f32[2048]{0:T(1024)}, u32[]{:S(2)}) copy-start(f32[2048]{0:T(1024)} %param.21) | copy-start | bytes 24580
  59.1 146.8 %all-gather.2.cloned.1.call-start = ((), (), s32[]{:S(2)}) async-start(), calls=%async_computation.4 | async-start | bytes 8650752 | tf_op jit(solution)/shard_map/all_gather | solution.py:99
  137.0 76.5 %copy-start.2 = (bf16[16,2048]{1,0:T(8,128)(2,1)}, bf16[16,2048]{1,0:T(8,128)(2,1)S(1)}, u32[]{:S(2)}) copy-start(bf16[16,2048]{1,0:T(8,128)(2,1)S(1)} %get-tuple-element.19) | copy-start | bytes 196612
  151.9 174.1 %reduce-scatter.2.cloned.1.call-start = ((), (), s32[]{:S(2)}) async-start(), calls=%async_computation.5 | async-start | bytes 8650752 | tf_op jit(solution)/shard_map/reduce_scatter | solution.py:104
  226.0 107.1 %copy-start.13 = (f32[16,2]{0,1:T(2,128)S(1)}, f32[16,2]{0,1:T(2,128)}, u32[]{:S(2)}) copy-start(f32[16,2]{0,1:T(2,128)} %param.23) | copy-start | bytes 388
  326.0 17.5 %all-to-all-start.1 = ((bf16[8,8,2048]{2,1,0:T(8,128)(2,1)}), bf16[8,8,2048]{2,1,0:T(8,128)(2,1)S(1)}, u32[]{:S(2)}, u32[]{:S(2)}) async-start(bf16[8,8,2048]{2,1,0:T(8,128)(2,1)} %bitcast.101), calls=%async_computation.2 | async-start | bytes 524288 | tf_op jit(solution)/shard_map/all_to_all | solution.py:110
Sparse Core Ops, SparseCore 0:
  59.2 76.6 all-reduce.1
  152.0 53.8 all-gather.1
  226.2 99.7 reduce-scatter.1
where the time goes:
time: 353 us; the launch traced here: 352 us
  waiting for transfers between devices  240 us (68%)
  matrix products  43 us (12%)
  local copies, waits for them, and re-layouts  20.2 us (6%)
  blocking collectives  14.4 us (4%)
  between operations  14.1 us (4%)
  other arithmetic  12.8 us (4%)
  starting transfers between devices  7.29 us (2%)
    reduce_scatter x1, waiting for transfers between devices, local(): lax.psum_scatter(jnp.dot(portion, w_down, preferred_element_type=jnp.floa...  99.6 us
    psum x1, waiting for transfers between devices, local(): lax.psum(partial_value.astype(jnp.bfloat16), 'exp').astype(jnp.float32)  76.3 us
    all_gather x1, waiting for transfers between devices, local(): portion = lax.all_gather(arrived, 'req', axis=0, tiled=True)  53.8 us
    all_to_all x1, blocking collectives, local(): lax.all_to_all(outgoing, 'exp', split_axis=0, concat_axis=0, tiled=True)  14.4 us
    dot_general x8, matrix products, local(): jnp.dot(chosen, out_weight[expert_index], preferred_element_type=jnp.floa...  13.2 us
    dot_general x1, matrix products, local(): jnp.dot(portion, w_down, preferred_element_type=jnp.float32)  12.5 us
    all_to_all x1, waiting for transfers between devices, local(): lax.all_to_all(returned, 'exp', split_axis=0, concat_axis=0, tiled=True)  10.3 us
    dot_general x1, matrix products, local(): gate_part = jnp.dot(portion, w_gate, preferred_element_type=jnp.float32)  7.55 us
  transfers between devices with their start and end apart: 4, of which 4 were waited for; matrix products, arithmetic and copies ran while one was open for 0% of the time, Pallas kernels for 0%

commit v1 on v0

v1 whole, which is shorter than its diff:
```python
import jax
import jax.numpy as jnp
from jax import lax
from jax.experimental import pallas as pl
from jax.experimental.pallas import tpu as pltpu
from jax.sharding import PartitionSpec as P

HD = 128
TOPA = 2
SPAN = 120
F32 = jnp.float32
BF16 = jnp.bfloat16
MESH = pl.DeviceIdType.MESH
VMEM_LIMIT = 60 * 1024 * 1024


def attention_kernel(
    table, lengths, q_ref, route_ref, gate_ref, kv_hbm, w_hbm, out_ref,
    kv, w, mix, x_rows, kv_sem, w_sem,
):
    pages = table.shape[1]
    decodes = table.shape[0] - 1
    page = kv.shape[2]
    experts = w.shape[0]
    width = q_ref.shape[2]
    tokens = q_ref.shape[1]
    head_count = width // HD
    copies = []
    for p in range(pages):
        copies.append(pltpu.make_async_copy(kv_hbm.at[table[0, p]], kv.at[p], kv_sem.at[p]))
    for s in range(decodes):
        copies.append(
            pltpu.make_async_copy(
                kv_hbm.at[table[s + 1, 0]], kv.at[pages + s], kv_sem.at[pages + s]
            )
        )
    for copy in copies:
        copy.start()
    w_copies = [pltpu.make_async_copy(w_hbm.at[e], w.at[e], w_sem.at[e]) for e in range(experts)]
    for copy in w_copies:
        copy.start()
    for copy in copies:
        copy.wait()

    def attend(q, k, v, allowed):
        scores = lax.dot_general(
            q, k, (((1,), (1,)), ((), ())), preferred_element_type=F32
        ) * HD ** (-0.5)
        scores = jnp.where(allowed, scores, -1e30)
        raised = jnp.exp(scores - jnp.max(scores, axis=1, keepdims=True))
        total = jnp.sum(raised, axis=1, keepdims=True)
        return jnp.dot(raised.astype(BF16), v, preferred_element_type=F32) / total

    keys = pages * page
    row_pos = lengths[0] - SPAN + lax.broadcasted_iota(jnp.int32, (tokens, keys), 0)
    causal = lax.broadcasted_iota(jnp.int32, (tokens, keys), 1) <= row_pos
    tail = 2 * decodes
    d_keys = decodes * page
    d_row = lax.broadcasted_iota(jnp.int32, (TOPA * tail, d_keys), 0) % tail - decodes
    d_col = lax.broadcasted_iota(jnp.int32, (TOPA * tail, d_keys), 1)
    d_slot = d_col // page
    length_of = jnp.zeros((TOPA * tail, d_keys), jnp.int32)
    for s in range(decodes):
        length_of = jnp.where(d_slot == s, lengths[s + 1], length_of)
    d_allowed = (d_slot == d_row) & (d_col % page < length_of)
    for h in range(head_count):
        cols = slice(h * HD, (h + 1) * HD)
        k_pre = kv[0:pages, 0, :, cols].reshape(keys, HD)
        v_pre = kv[0:pages, 1, :, cols].reshape(keys, HD)
        for t in range(TOPA):
            mix[t, :, cols] = attend(q_ref[t, :, cols], k_pre, v_pre, causal)
        k_dec = kv[pages : pages + decodes, 0, :, cols].reshape(d_keys, HD)
        v_dec = kv[pages : pages + decodes, 1, :, cols].reshape(d_keys, HD)
        q_dec = jnp.concatenate(
            [q_ref[t, tokens - tail : tokens, cols] for t in range(TOPA)], axis=0
        )
        o_dec = attend(q_dec, k_dec, v_dec, d_allowed)
        for t in range(TOPA):
            mix[t, SPAN:tokens, cols] = o_dec[t * tail + decodes : (t + 1) * tail]
    mixes = [mix[t].astype(BF16).astype(F32) for t in range(TOPA)]
    routes = [route_ref[:, t : t + 1] for t in range(TOPA)]
    gates = [gate_ref[:, t : t + 1] for t in range(TOPA)]
    for e in range(experts):
        gated = jnp.zeros((tokens, width), F32)
        for t in range(TOPA):
            gated = gated + jnp.where(routes[t] == e, gates[t], 0.0) * mixes[t]
        x_rows[:, e * width : (e + 1) * width] = gated.astype(BF16)
    for copy in w_copies:
        copy.wait()
    outs = w.shape[2]
    step = 512
    for n in range(0, outs, step):
        out_ref[:, n : n + step] = jnp.dot(
            x_rows[...],
            w[:, :, n : n + step].reshape(experts * width, step),
            preferred_element_type=F32,
        ).astype(BF16)


def attention(table, lengths, q, route, gate, kv_cache, out_weight):
    pool, _, page, width = kv_cache.shape
    experts, _, outs = out_weight.shape
    tokens = q.shape[1]
    vmem = pl.BlockSpec(memory_space=pltpu.VMEM)
    smem = pl.BlockSpec(memory_space=pltpu.SMEM)
    hbm = pl.BlockSpec(memory_space=pl.ANY)
    slots = table.shape[1] + table.shape[0] - 1
    return pl.pallas_call(
        attention_kernel,
        out_shape=jax.ShapeDtypeStruct((tokens, outs), BF16),
        in_specs=[smem, smem, vmem, vmem, vmem, hbm, hbm],
        out_specs=vmem,
        scratch_shapes=[
            pltpu.VMEM((slots, 2, page, width), BF16),
            pltpu.VMEM((experts, width, outs), BF16),
            pltpu.VMEM((TOPA, tokens, width), F32),
            pltpu.VMEM((tokens, experts * width), BF16),
            pltpu.SemaphoreType.DMA((slots,)),
            pltpu.SemaphoreType.DMA((experts,)),
        ],
        compiler_params=pltpu.CompilerParams(vmem_limit_bytes=VMEM_LIMIT),
        name="attention",
    )(table, lengths, q, route, gate, kv_cache, out_weight)


def layer_kernel(
    partial, residual, gain, route, egate, g_hbm, u_hbm, d_hbm, attended_ref, mix_ref,
    rs_buf, out_buf, in_buf, ra, rb, wg, wu, wd, act, pa, pb,
    ta1, ta2, sa, ta3, tb1, tb2, tb3, ret_out, ret_in,
    z_send, z_recv, ag_send, ag_recv, rs_send, rs_recv, w_send, w_recv, l_sem,
):
    nz = partial.shape[0]
    rows = residual.shape[0]
    cap = out_buf.shape[1]
    block = nz * cap
    half_cols = ra.shape[3]
    hidden = g_hbm.shape[0]
    me = lax.axis_index("req")
    z = lax.axis_index("exp")
    c = lax.rem(me, 2)
    y = lax.rem(lax.div(me, 2), 4)
    x = lax.div(me, 8)
    xp, xm, x2 = lax.rem(x + 1, 4), lax.rem(x + 3, 4), lax.rem(x + 2, 4)
    yw = y + 1 - 2 * lax.rem(y, 2)
    turned = lax.rem(y + 3, 4)
    ys = lax.rem(turned, 2)
    yo = 1 - ys
    yr = lax.rem(turned + 1 - 2 * ys + 1, 4)

    def dev(x_, y_, c_):
        return ((x_ * 4 + y_) * 2 + c_, z)

    right, left = dev(xp, y, c), dev(xm, y, c)
    pair = dev(x, yr, c)
    w_pair = dev(x, yw, c)
    core = dev(x, y, 1 - c)

    def ahead(d):
        return (me, lax.rem(z + d, nz))

    def behind(d):
        return (me, lax.rem(z + nz - d, nz))

    barrier = pltpu.get_barrier_semaphore()
    others = [ahead(d) for d in range(1, nz)] + [right, left, pair, w_pair, core]
    for other in others:
        pl.semaphore_signal(barrier, inc=1, device_id=other, device_id_type=MESH)
    pl.semaphore_wait(barrier, len(others))

    started = []

    def send(src, dst, sems, i, device):
        copy = pltpu.make_async_remote_copy(
            src_ref=src, dst_ref=dst, send_sem=sems[0].at[i], recv_sem=sems[1].at[i],
            device_id=device, device_id_type=MESH,
        )
        copy.start()
        started.append(copy)
        return copy

    zs, ags, rss, ws = (z_send, z_recv), (ag_send, ag_recv), (rs_send, rs_recv), (w_send, w_recv)

    scatter = [
        send(partial.at[lax.rem(z + d, nz)], rs_buf.at[d - 1], zs, d - 1, ahead(d))
        for d in (4, 3, 5, 2, 6, 1, 7)
    ]
    sources, stores = (g_hbm, u_hbm, d_hbm), (wg, wu, wd)

    def part(store, b):
        return store.at[pl.ds(b * hidden, hidden)]

    w_y = [send(sources[i], part(stores[i], 1), ws, i, w_pair) for i in range(3)]
    w_c = [send(sources[i], part(stores[i], 2), ws, 3 + i, core) for i in range(3)]
    w_l = [
        pltpu.make_async_copy(sources[i], part(stores[i], 0), l_sem.at[i]) for i in range(3)
    ]
    for copy in w_l:
        copy.start()

    def routed(t):
        rel = route[:, t : t + 1] - z
        rel = jnp.where(rel < 0, rel + nz, rel)
        return rel == lax.broadcasted_iota(jnp.int32, (rows, block), 1) // cap

    named = [routed(t) for t in range(TOPA)]
    member = jnp.where(named[0] | named[1], 1.0, 0.0).astype(F32)
    lower = jnp.where(
        lax.broadcasted_iota(jnp.int32, (rows, rows), 1)
        < lax.broadcasted_iota(jnp.int32, (rows, rows), 0),
        1.0, 0.0,
    ).astype(BF16)
    rank = jnp.dot(lower, member.astype(BF16), preferred_element_type=F32)
    place = (lax.broadcasted_iota(jnp.int32, (rows, block), 1) % cap).astype(F32)
    placing = jnp.where(rank == place, member, 0.0)

    for copy in scatter:
        copy.wait_recv()
    summed = residual[...].astype(F32) + partial[z].astype(F32)
    for d in range(nz - 1):
        summed = summed + rs_buf[d].astype(F32)
    attended = summed.astype(BF16)
    attended_ref[...] = attended
    values = attended.astype(F32)
    normed = (
        values
        * lax.rsqrt(jnp.mean(values * values, axis=1, keepdims=True) + 1e-06)
        * gain[...]
    ).astype(BF16)
    outgoing = lax.dot_general(
        placing.astype(BF16), normed, (((0,), (0,)), ((), ())), preferred_element_type=F32
    )
    for d in range(nz):
        out_buf[d] = outgoing[d * cap : (d + 1) * cap].astype(BF16)
    dispatch = [
        send(out_buf.at[d], in_buf.at[d - 1], zs, 6 + d, ahead(d)) for d in (4, 3, 5, 2, 6, 1, 7)
    ]
    for copy in dispatch:
        copy.wait_recv()
    arrived = jnp.concatenate(
        [out_buf[0].astype(F32)] + [in_buf[d].astype(F32) for d in range(nz - 1)], axis=0
    ).astype(BF16)

    ra[ys, x] = arrived[:, :half_cols]
    rb[ys, x] = arrived[:, half_cols:]
    mid = block // 2
    a_y = send(ra.at[ys, x], ra.at[ys, x], ags, 0, pair)
    b_r = send(rb.at[ys, x], rb.at[ys, x], ags, 1, right)
    b_l = send(rb.at[ys, x], rb.at[ys, x], ags, 2, left)
    a_y.wait_recv()
    a_r = send(ra.at[:, x], ra.at[:, x], ags, 3, right)
    a_l = send(ra.at[:, x], ra.at[:, x], ags, 4, left)
    b_r.wait_recv()
    b_r2 = send(rb.at[ys, xm, pl.ds(0, mid)], rb.at[ys, xm, pl.ds(0, mid)], ags, 5, right)
    b_l.wait_recv()
    b_l2 = send(rb.at[ys, xp, pl.ds(mid, mid)], rb.at[ys, xp, pl.ds(mid, mid)], ags, 6, left)
    b_r2.wait_recv()
    b_l2.wait_recv()
    b_y = send(rb.at[ys], rb.at[ys], ags, 7, pair)
    a_r.wait_recv()
    a_r2 = send(ra.at[0, xm], ra.at[0, xm], ags, 8, right)
    a_l.wait_recv()
    a_l2 = send(ra.at[1, xp], ra.at[1, xp], ags, 9, left)
    w_d = []
    for i in range(3):
        w_y[i].wait_recv()
        w_d.append(send(part(stores[i], 1), part(stores[i], 3), ws, 6 + i, core))
    a_r2.wait_recv()
    a_l2.wait_recv()
    b_y.wait_recv()
    for i in range(3):
        w_c[i].wait_recv()
        w_d[i].wait_recv()
        w_l[i].wait()

    amount = act.shape[0]
    xa = ra[...].reshape(amount, half_cols)
    xb = rb[...].reshape(amount, half_cols)

    def wide(x_half, w_half):
        return lax.dot_general(
            x_half, w_half, (((1,), (1,)), ((), ())), preferred_element_type=F32
        )

    units = act.shape[1]
    step = 256
    for n in range(0, units, step):
        width = min(step, units - n)
        gate_part = wide(xa, wg[n : n + width, :half_cols]) + wide(xb, wg[n : n + width, half_cols:])
        up_part = wide(xa, wu[n : n + width, :half_cols]) + wide(xb, wu[n : n + width, half_cols:])
        act[:, n : n + width] = (
            gate_part / (1.0 + jnp.exp(-gate_part)) * up_part
        ).astype(BF16)
    for n in range(0, half_cols, step):
        for store, base in ((pa, 0), (pb, half_cols)):
            store[:, :, :, n : n + step] = jnp.dot(
                act[...], wd[:, base + n : base + n + step], preferred_element_type=F32
            ).astype(BF16).reshape(2, 4, block, step)

    b1 = send(pb.at[yo], tb1, rss, 0, pair)
    a1r = send(pa.at[0, x2], ta1.at[0], rss, 1, right)
    a1l = send(pa.at[1, x2], ta1.at[1], rss, 2, left)
    a1r.wait_recv()
    pa[0, xp] = (pa[0, xp].astype(F32) + ta1[0].astype(F32)).astype(BF16)
    a2r = send(pa.at[:, xp], ta2.at[0], rss, 3, right)
    a1l.wait_recv()
    pa[1, xm] = (pa[1, xm].astype(F32) + ta1[1].astype(F32)).astype(BF16)
    a2l = send(pa.at[:, xm], ta2.at[1], rss, 4, left)
    b1.wait_recv()
    pb[ys, x2] = (pb[ys, x2].astype(F32) + tb1[x2].astype(F32)).astype(BF16)
    b2r = send(pb.at[ys, x2, pl.ds(0, mid)], tb2.at[0], rss, 5, right)
    b2l = send(pb.at[ys, x2, pl.ds(mid, mid)], tb2.at[1], rss, 6, left)
    for spot in (xp, xm):
        pb[ys, spot] = (pb[ys, spot].astype(F32) + tb1[spot].astype(F32)).astype(BF16)
    a2r.wait_recv()
    a2l.wait_recv()
    for k in range(2):
        sa[k] = (
            pa[k, x].astype(F32) + ta2[0, k].astype(F32) + ta2[1, k].astype(F32)
        ).astype(BF16)
    a3 = send(sa.at[yo], ta3, rss, 7, pair)
    b2r.wait_recv()
    pb[ys, xp, 0:mid] = (pb[ys, xp, 0:mid].astype(F32) + tb2[0].astype(F32)).astype(BF16)
    b3r = send(pb.at[ys, xp], tb3.at[0], rss, 8, right)
    b2l.wait_recv()
    pb[ys, xm, mid:block] = (pb[ys, xm, mid:block].astype(F32) + tb2[1].astype(F32)).astype(BF16)
    b3l = send(pb.at[ys, xm], tb3.at[1], rss, 9, left)
    own_b = pb[ys, x].astype(F32) + tb1[x].astype(F32)
    a3.wait_recv()
    final_a = sa[ys].astype(F32) + ta3[...].astype(F32)
    b3r.wait_recv()
    b3l.wait_recv()
    final_b = own_b + tb3[0].astype(F32) + tb3[1].astype(F32)

    for d in range(nz):
        ret_out[d, :, :half_cols] = final_a[d * cap : (d + 1) * cap].astype(BF16)
        ret_out[d, :, half_cols:] = final_b[d * cap : (d + 1) * cap].astype(BF16)
    home = [
        send(ret_out.at[d], ret_in.at[d - 1], zs, 13 + d, behind(d)) for d in (4, 3, 5, 2, 6, 1, 7)
    ]
    weights = jnp.where(named[0], egate[:, 0:1], 0.0) + jnp.where(named[1], egate[:, 1:2], 0.0)
    weights = placing * weights
    high = weights.astype(BF16)
    low = (weights - high.astype(F32)).astype(BF16)
    both = jnp.concatenate([high, low], axis=0)
    for copy in home:
        copy.wait_recv()
    back = jnp.concatenate(
        [ret_out[0].astype(F32)] + [ret_in[d].astype(F32) for d in range(nz - 1)], axis=0
    ).astype(BF16)
    mixed = jnp.dot(both, back, preferred_element_type=F32)
    mix_ref[...] = (mixed[:rows] + mixed[rows:]).astype(BF16)
    for copy in started:
        copy.wait_send()


def moe_layer(partial, residual, gain, route, egate, g_t, u_t, down):
    nz, rows, width = partial.shape
    half_cols = width // 2
    hidden = g_t.shape[0]
    cap = max(2, 2 * TOPA * rows // nz)
    block = nz * cap
    amount = 8 * block
    units = 4 * hidden
    vmem = pl.BlockSpec(memory_space=pltpu.VMEM)
    hbm = pl.BlockSpec(memory_space=pl.ANY)

    def buf(*shape):
        return pltpu.VMEM(shape, BF16)

    def dma(n):
        return pltpu.SemaphoreType.DMA((n,))

    return pl.pallas_call(
        layer_kernel,
        out_shape=(
            jax.ShapeDtypeStruct((rows, width), BF16),
            jax.ShapeDtypeStruct((rows, width), BF16),
        ),
        in_specs=[vmem] * 5 + [hbm] * 3,
        out_specs=(vmem, vmem),
        scratch_shapes=[
            buf(nz - 1, rows, width),
            buf(nz, cap, width),
            buf(nz - 1, cap, width),
            buf(2, 4, block, half_cols),
            buf(2, 4, block, half_cols),
            buf(units, width),
            buf(units, width),
            buf(units, width),
            buf(amount, units),
            buf(2, 4, block, half_cols),
            buf(2, 4, block, half_cols),
            buf(2, block, half_cols),
            buf(2, 2, block, half_cols),
            buf(2, block, half_cols),
            buf(block, half_cols),
            buf(4, block, half_cols),
            buf(2, block // 2, half_cols),
            buf(2, block, half_cols),
            buf(nz, cap, width),
            buf(nz - 1, cap, width),
            dma(3 * (nz - 1)), dma(3 * (nz - 1)),
            dma(10), dma(10), dma(10), dma(10), dma(9), dma(9), dma(3),
        ],
        compiler_params=pltpu.CompilerParams(
            collective_id=0, has_side_effects=True, vmem_limit_bytes=VMEM_LIMIT
        ),
        name="moe_layer",
    )(partial, residual, gain, route, egate, g_t, u_t, down)


def local(
    residual, queries, kv_cache, page_table, seq_lengths, head_route, head_gate, out_weight,
    norm_gain, expert_route, expert_gate, gate_up, down_weight,
):
    turned = jnp.transpose(gate_up[0], (0, 2, 1))
    partial = attention(
        page_table, seq_lengths, jnp.transpose(queries, (1, 0, 2)), head_route, head_gate,
        kv_cache, out_weight,
    )
    rows, width = residual.shape
    return moe_layer(
        partial.reshape(-1, rows, width), residual, norm_gain.reshape(1, -1), expert_route,
        expert_gate, turned[0], turned[1], down_weight[0],
    )


def solution(mesh):
    return jax.shard_map(
        local,
        mesh=mesh,
        in_specs=(
            P(("req", "exp"), None),
            P("req", None, "exp"),
            P("req", None, None, "exp"),
            P("req", None),
            P("req"),
            P("req", None),
            P("req", None),
            P(None, "exp", None),
            P(),
            P(("req", "exp"), None),
            P(("req", "exp"), None),
            P("exp", None, None, "req"),
            P("exp", "req", None),
        ),
        out_specs=(P(("req", "exp"), None), P(("req", "exp"), None)),
        check_vma=False,
    )
```

time: 353 us -> 118 us (0.33)
  waiting for transfers between devices: 240 us -> 0 us
  Pallas kernels: 0 us -> 105 us
  matrix products: 43 us -> 0 us
  blocking collectives: 14.4 us -> 0 us
  between operations: 14.1 us -> 0.66 us
  other arithmetic: 12.8 us -> 0 us
  local copies, waits for them, and re-layouts: 20.2 us -> 11.3 us
  starting transfers between devices: 7.29 us -> 0 us
    pallas_call x0 -> x2, Pallas kernels: none -> 105 us  [the longest x1 95.6 us: moe_layer(): pl.pallas_call(layer_kernel, out_shape=(jax.ShapeDtypeStruct((rows, width...]
    reduce_scatter x1 -> x0, waiting for transfers between devices: 99.6 us -> none  [local(): lax.psum_scatter(jnp.dot(portion, w_down, preferred_element_type=jnp.floa...]
    psum x1 -> x0, waiting for transfers between devices: 76.3 us -> none  [local(): lax.psum(partial_value.astype(jnp.bfloat16), 'exp').astype(jnp.float32)]
    all_gather x1 -> x0, waiting for transfers between devices: 53.8 us -> none  [local(): portion = lax.all_gather(arrived, 'req', axis=0, tiled=True)]
    dot_general x13 -> x0, matrix products: 36.9 us -> none  [the longest x8 13.2 us: local(): jnp.dot(chosen, out_weight[expert_index], preferred_element_type=jnp.floa...]
    all_to_all x1 -> x0, blocking collectives: 14.4 us -> none  [local(): lax.all_to_all(outgoing, 'exp', split_axis=0, concat_axis=0, tiled=True)]
    all_to_all x1 -> x0, waiting for transfers between devices: 10.3 us -> none  [local(): lax.all_to_all(returned, 'exp', split_axis=0, concat_axis=0, tiled=True)]
    unnamed x32 -> x9, local copies, waits for them, and re-layouts: 0.24 us -> 10 us
  transfers between devices with their start and end apart: 4 -> 0, of which waited for: 4 -> 0; matrix products, arithmetic and copies ran while one was open for 0% -> 0% of each run, Pallas kernels for 0% -> 0%
where the time goes in v1:
time: 118 us; the launch traced here: 117 us
  Pallas kernels  105 us (89%)
  local copies, waits for them, and re-layouts  11.3 us (10%)
    pallas_call x1, Pallas kernels, moe_layer(): pl.pallas_call(layer_kernel, out_shape=(jax.ShapeDtypeStruct((rows, width...  95.6 us
    unnamed x9, local copies, waits for them, and re-layouts  10 us
    pallas_call x1, Pallas kernels, attention(): pl.pallas_call(attention_kernel, out_shape=jax.ShapeDtypeStruct((tokens,...  9.83 us

profile of v1, /device:TPU:2, one launch (start us, length us, event | category | flops | bytes accessed | tf_op | source)
XLA Modules:
  0.0 117.4 jit_solution(10306459130846659044)
XLA Ops:
  0.6 1.3 %copy.18.route = s32[16,2]{1,0:T(8,128)} copy(s32[16,2]{0,1:T(2,128)} %param.22) | data formatting | bytes 256 | tf_op args[9]
  2.0 1.4 %copy.19.egate = f32[16,2]{1,0:T(8,128)} copy(f32[16,2]{0,1:T(2,128)} %param.23) | data formatting | bytes 256 | tf_op args[10]
  3.3 1.4 %copy.16.route_ref = s32[128,2]{1,0:T(8,128)} copy(s32[128,2]{0,1:T(2,128)} %param.18) | data formatting | bytes 2048 | tf_op args[5]
  4.7 1.4 %copy.17.gate_ref = f32[128,2]{1,0:T(8,128)} copy(f32[128,2]{0,1:T(2,128)} %param.19) | data formatting | bytes 2048 | tf_op args[6]
  6.2 1.6 %copy.21 = bf16[128,2,256]{2,0,1:T(8,128)(2,1)} copy(bf16[128,2,256]{2,1,0:T(2,128)(2,1)} %param.14) | data formatting | bytes 262144 | tf_op args[1]
  7.7 0.0 copy-start
  7.7 9.8 %attention.1 = bf16[128,2048]{1,0:T(8,128)(2,1)} custom-call(s32[9,11]{1,0:T(8,128)} %table.1, s32[9]{0:T(128)} %lengths.1, bf16[2,128,256]{2,1,0:T(8,128)(2,1)} %bitcast.16, s32[128,2]{1,0:T(8,128)} %copy.16.route_ref, f32[128,2]{1,0:T(8,128)} %copy.17.gate_ref, bf16[19,2,128,256]{3,2,1,0:T(8,128)(2,1)} %kv_hbm.1, bf16[8,256,2048]{2,1,0:T(8,128)(2,1)} %w_hbm.1), custom_call_target="tpu_custom_call" | custom-call | tf_op jit(solution)/shard_map/attention/pallas_call | solution.py:108
  17.6 0.0 copy-done
  17.6 1.3 %slice_bitcast_fusion = (bf16[176,2048]{1,0:T(8,128)(2,1)}, bf16[176,2048]{1,0:T(8,128)(2,1)}) fusion(bf16[2,176,2048]{2,1,0:T(8,128)(2,1)S(1)} %bitcast.14), kind=kLoop, calls=%fused_computation | loop fusion | bytes 2883584 | tf_op jit(solution)/shard_map/squeeze | solution.py:424
  18.9 95.6 %moe_layer.1 = (bf16[16,2048]{1,0:T(8,128)(2,1)}, bf16[16,2048]{1,0:T(8,128)(2,1)}) custom-call(bf16[8,16,2048]{2,1,0:T(8,128)(2,1)} %bitcast.13, bf16[16,2048]{1,0:T(8,128)(2,1)} %residual.1, f32[1,2048]{1,0:T(1,128)} %bitcast.17, s32[16,2]{1,0:T(8,128)} %copy.18.route, f32[16,2]{1,0:T(8,128)} %copy.19.egate, bf16[176,2048]{1,0:T(8,128)(2,1)} %get-tuple-element.3.g_hbm, ...), custom_call_target="tpu_custom_call" | custom-call | tf_op jit(solution)/shard_map/moe_layer/pallas_call | solution.py:373
  114.4 1.5 %copy.24 = bf16[16,2048]{1,0:T(8,128)(2,1)} copy(bf16[16,2048]{1,0:T(8,128)(2,1)} %get-tuple-element.6) | data formatting | bytes 131072
  115.9 1.5 %copy.25 = bf16[16,2048]{1,0:T(8,128)(2,1)} copy(bf16[16,2048]{1,0:T(8,128)(2,1)} %get-tuple-element.7) | data formatting | bytes 131072
Async XLA Ops:
  7.7 9.8 %copy-start = (bf16[1,2,2048,176]{2,3,1,0:T(8,128)(2,1)S(1)}, bf16[1,2,2048,176]{2,3,1,0:T(8,128)(2,1)}, u32[]{:S(2)}) copy-start(bf16[1,2,2048,176]{2,3,1,0:T(8,128)(2,1)} %param.24) | copy-start | bytes 4325380

commit v2 on v1

v2 whole, which is shorter than its diff:
```python
import jax
import jax.numpy as jnp
from jax import lax
from jax.experimental import pallas as pl
from jax.experimental.pallas import tpu as pltpu
from jax.sharding import PartitionSpec as P

HD = 128
TOPA = 2
SPAN = 120
F32 = jnp.float32
BF16 = jnp.bfloat16
MESH = pl.DeviceIdType.MESH
VMEM_LIMIT = 60 * 1024 * 1024


def column(row):
    n = row.shape[1]
    same = lax.broadcasted_iota(jnp.int32, (n, n), 0) == lax.broadcasted_iota(jnp.int32, (n, n), 1)
    return jnp.sum(jnp.where(same, jnp.broadcast_to(row, (n, n)), 0.0), axis=1, keepdims=True)


def attend(q, k, v, allowed):
    scores = lax.dot_general(
        q, k, (((1,), (1,)), ((), ())), preferred_element_type=F32
    ) * HD ** (-0.5)
    scores = jnp.where(allowed, scores, -1e30)
    raised = jnp.exp(scores - jnp.max(scores, axis=1, keepdims=True))
    total = jnp.sum(raised, axis=1, keepdims=True)
    return jnp.dot(raised.astype(BF16), v, preferred_element_type=F32) / total


def layer_kernel(
    table, lengths, q_ref, head_route, head_gate, residual, gain, route, egate,
    kv_hbm, w_hbm, gu_hbm, d_hbm, attended_ref, mix_ref,
    kv, w, mix, x_rows, partial, rs_buf, out_buf, in_buf, ra, rb, wg, wu, wd, act, pa, pb,
    ta1, ta2, sa, ta3, tb1, tb2, tb3, ret_out, ret_in,
    kv_sem, o_sem, s_send, s_recv, z_send, z_recv, ag_send, ag_recv, rs_send, rs_recv,
    w_send, w_recv, l_sem,
):
    nz = partial.shape[0]
    rows = residual.shape[0]
    cap = out_buf.shape[1]
    block = nz * cap
    half_cols = ra.shape[3]
    hidden = d_hbm.shape[0]
    me = lax.axis_index("req")
    z = lax.axis_index("exp")
    c = lax.rem(me, 2)
    y = lax.rem(lax.div(me, 2), 4)
    x = lax.div(me, 8)
    xp, xm, x2 = lax.rem(x + 1, 4), lax.rem(x + 3, 4), lax.rem(x + 2, 4)
    yw = y + 1 - 2 * lax.rem(y, 2)
    turned = lax.rem(y + 3, 4)
    ys = lax.rem(turned, 2)
    yo = 1 - ys
    yr = lax.rem(turned + 1 - 2 * ys + 1, 4)

    def dev(x_, y_, c_):
        return ((x_ * 4 + y_) * 2 + c_, z)

    right, left = dev(xp, y, c), dev(xm, y, c)
    pair = dev(x, yr, c)
    w_pair = dev(x, yw, c)
    core = dev(x, y, 1 - c)

    def ahead(d):
        return (me, lax.rem(z + d, nz))

    def behind(d):
        return (me, lax.rem(z + nz - d, nz))

    barrier = pltpu.get_barrier_semaphore()
    others = [ahead(d) for d in range(1, nz)] + [right, left, pair, w_pair, core]
    for other in others:
        pl.semaphore_signal(barrier, inc=1, device_id=other, device_id_type=MESH)
    kv_copy = pltpu.make_async_copy(kv_hbm, kv, kv_sem.at[0])
    kv_copy.start()
    experts = w.shape[0]
    o_copies = [pltpu.make_async_copy(w_hbm.at[e], w.at[e], o_sem.at[e]) for e in range(experts)]
    for copy in o_copies:
        copy.start()
    pl.semaphore_wait(barrier, len(others))

    started = []

    def send(src, dst, sems, i, device):
        copy = pltpu.make_async_remote_copy(
            src_ref=src, dst_ref=dst, send_sem=sems[0].at[i], recv_sem=sems[1].at[i],
            device_id=device, device_id_type=MESH,
        )
        copy.start()
        started.append(copy)
        return copy

    zs, ags, rss, ws = (z_send, z_recv), (ag_send, ag_recv), (rs_send, rs_recv), (w_send, w_recv)
    ss = (s_send, s_recv)
    far_first = (4, 3, 5, 2, 6, 1, 7)

    sources, stores = (gu_hbm.at[0], gu_hbm.at[1], d_hbm), (wg, wu, wd)

    def part(store, b):
        return store.at[pl.ds(b * hidden, hidden)]

    w_y = [send(sources[i], part(stores[i], 1), ws, i, w_pair) for i in range(3)]
    w_c = [send(sources[i], part(stores[i], 2), ws, 3 + i, core) for i in range(3)]
    w_l = [
        pltpu.make_async_copy(sources[i], part(stores[i], 0), l_sem.at[i]) for i in range(3)
    ]
    for copy in w_l:
        copy.start()

    pages = table.shape[1]
    decodes = table.shape[0] - 1
    page = kv.shape[2]
    width = q_ref.shape[2]
    tokens = q_ref.shape[1]
    keys = pages * page
    row_pos = lengths[0] - SPAN + lax.broadcasted_iota(jnp.int32, (tokens, keys), 0)
    causal = lax.broadcasted_iota(jnp.int32, (tokens, keys), 1) <= row_pos
    tail = 2 * decodes
    d_keys = decodes * page
    d_row = lax.broadcasted_iota(jnp.int32, (TOPA * tail, d_keys), 0) % tail - decodes
    d_col = lax.broadcasted_iota(jnp.int32, (TOPA * tail, d_keys), 1)
    d_slot = d_col // page
    length_of = jnp.zeros((TOPA * tail, d_keys), jnp.int32)
    for s in range(decodes):
        length_of = jnp.where(d_slot == s, lengths[s + 1], length_of)
    d_allowed = (d_slot == d_row) & (d_col % page < length_of)
    kv_copy.wait()
    for h in range(width // HD):
        cols = slice(h * HD, (h + 1) * HD)

        def paged(kind, spots):
            return jnp.concatenate([kv[table[s, p], kind, :, cols] for s, p in spots], axis=0)

        pre = [(0, p) for p in range(pages)]
        k_pre, v_pre = paged(0, pre), paged(1, pre)
        for t in range(TOPA):
            mix[t, :, cols] = attend(q_ref[t, :, cols], k_pre, v_pre, causal)
        dec = [(s + 1, 0) for s in range(decodes)]
        k_dec, v_dec = paged(0, dec), paged(1, dec)
        q_dec = jnp.concatenate(
            [q_ref[t, tokens - tail : tokens, cols] for t in range(TOPA)], axis=0
        )
        o_dec = attend(q_dec, k_dec, v_dec, d_allowed)
        for t in range(TOPA):
            mix[t, SPAN:tokens, cols] = o_dec[t * tail + decodes : (t + 1) * tail]
    mixes = [mix[t].astype(BF16).astype(F32) for t in range(TOPA)]
    routes = [column(head_route[t : t + 1].astype(F32)) for t in range(TOPA)]
    gates = [column(head_gate[t : t + 1]) for t in range(TOPA)]
    for e in range(experts):
        gated = jnp.zeros((tokens, width), F32)
        for t in range(TOPA):
            gated = gated + jnp.where(routes[t] == e, gates[t], 0.0) * mixes[t]
        x_rows[:, e * width : (e + 1) * width] = gated.astype(BF16)
    for copy in o_copies:
        copy.wait()

    outs = w.shape[2]
    chunk = outs // 4
    scatter = []
    for n in range(0, outs, chunk):
        partial[:, :, n : n + chunk] = jnp.dot(
            x_rows[...],
            w[:, :, n : n + chunk].reshape(experts * width, chunk),
            preferred_element_type=F32,
        ).astype(BF16).reshape(nz, rows, chunk)
        for d in far_first:
            scatter.append(
                send(
                    partial.at[lax.rem(z + d, nz), :, pl.ds(n, chunk)],
                    rs_buf.at[d - 1, :, pl.ds(n, chunk)],
                    ss, (n // chunk) * (nz - 1) + d - 1, ahead(d),
                )
            )

    def routed(t):
        rel = column(route[t : t + 1].astype(F32)) - z.astype(F32)
        rel = jnp.where(rel < 0, rel + nz, rel)
        spot = lax.broadcasted_iota(jnp.int32, (rows, block), 1) // cap
        return rel == spot.astype(F32)

    named = [routed(t) for t in range(TOPA)]
    member = jnp.where(named[0] | named[1], 1.0, 0.0).astype(F32)
    lower = jnp.where(
        lax.broadcasted_iota(jnp.int32, (rows, rows), 1)
        < lax.broadcasted_iota(jnp.int32, (rows, rows), 0),
        1.0, 0.0,
    ).astype(BF16)
    rank = jnp.dot(lower, member.astype(BF16), preferred_element_type=F32)
    place = (lax.broadcasted_iota(jnp.int32, (rows, block), 1) % cap).astype(F32)
    placing = jnp.where(rank == place, member, 0.0)
    egates = [column(egate[t : t + 1]) for t in range(TOPA)]

    for copy in scatter:
        copy.wait_recv()
    summed = residual[...].astype(F32) + partial[z].astype(F32)
    for d in range(nz - 1):
        summed = summed + rs_buf[d].astype(F32)
    attended = summed.astype(BF16)
    attended_ref[...] = attended
    values = attended.astype(F32)
    normed = (
        values
        * lax.rsqrt(jnp.mean(values * values, axis=1, keepdims=True) + 1e-06)
        * gain[...]
    ).astype(BF16)
    outgoing = lax.dot_general(
        placing.astype(BF16), normed, (((0,), (0,)), ((), ())), preferred_element_type=F32
    )
    for d in range(nz):
        out_buf[d] = outgoing[d * cap : (d + 1) * cap].astype(BF16)
    dispatch = [
        send(out_buf.at[d], in_buf.at[d - 1], zs, d - 1, ahead(d)) for d in far_first
    ]
    for copy in dispatch:
        copy.wait_recv()
    arrived = jnp.concatenate(
        [out_buf[0].astype(F32)] + [in_buf[d].astype(F32) for d in range(nz - 1)], axis=0
    ).astype(BF16)

    ra[ys, x] = arrived[:, :half_cols]
    rb[ys, x] = arrived[:, half_cols:]
    mid = block // 2
    a_y = send(ra.at[ys, x], ra.at[ys, x], ags, 0, pair)
    b_r = send(rb.at[ys, x], rb.at[ys, x], ags, 1, right)
    b_l = send(rb.at[ys, x], rb.at[ys, x], ags, 2, left)
    a_y.wait_recv()
    a_r = send(ra.at[:, x], ra.at[:, x], ags, 3, right)
    a_l = send(ra.at[:, x], ra.at[:, x], ags, 4, left)
    b_r.wait_recv()
    b_r2 = send(rb.at[ys, xm, pl.ds(0, mid)], rb.at[ys, xm, pl.ds(0, mid)], ags, 5, right)
    b_l.wait_recv()
    b_l2 = send(rb.at[ys, xp, pl.ds(mid, mid)], rb.at[ys, xp, pl.ds(mid, mid)], ags, 6, left)
    b_r2.wait_recv()
    b_l2.wait_recv()
    b_y = send(rb.at[ys], rb.at[ys], ags, 7, pair)
    a_r.wait_recv()
    a_r2 = send(ra.at[0, xm], ra.at[0, xm], ags, 8, right)
    a_l.wait_recv()
    a_l2 = send(ra.at[1, xp], ra.at[1, xp], ags, 9, left)
    w_d = []
    for i in range(2):
        w_y[i].wait_recv()
        w_d.append(send(part(stores[i], 1), part(stores[i], 3), ws, 6 + i, core))
    a_r2.wait_recv()
    a_l2.wait_recv()
    b_y.wait_recv()
    for i in range(2):
        w_c[i].wait_recv()
        w_d[i].wait_recv()
        w_l[i].wait()

    amount = act.shape[0]
    xa = ra[...].reshape(amount, half_cols)
    xb = rb[...].reshape(amount, half_cols)

    def wide(x_half, w_half):
        return lax.dot_general(
            x_half, w_half, (((1,), (1,)), ((), ())), preferred_element_type=F32
        )

    units = act.shape[1]
    step = 256
    for n in range(0, units, step):
        size = min(step, units - n)
        gate_part = wide(xa, wg[n : n + size, :half_cols]) + wide(xb, wg[n : n + size, half_cols:])
        up_part = wide(xa, wu[n : n + size, :half_cols]) + wide(xb, wu[n : n + size, half_cols:])
        act[:, n : n + size] = (
            gate_part / (1.0 + jnp.exp(-gate_part)) * up_part
        ).astype(BF16)
    w_y[2].wait_recv()
    w_d.append(send(part(wd, 1), part(wd, 3), ws, 8, core))
    w_c[2].wait_recv()
    w_l[2].wait()
    w_d[2].wait_recv()
    for n in range(0, half_cols, step):
        for store, base in ((pa, 0), (pb, half_cols)):
            store[:, :, :, n : n + step] = jnp.dot(
                act[...], wd[:, base + n : base + n + step], preferred_element_type=F32
            ).astype(BF16).reshape(2, 4, block, step)

    b1 = send(pb.at[yo], tb1, rss, 0, pair)
    a1r = send(pa.at[0, x2], ta1.at[0], rss, 1, right)
    a1l = send(pa.at[1, x2], ta1.at[1], rss, 2, left)
    a1r.wait_recv()
    pa[0, xp] = (pa[0, xp].astype(F32) + ta1[0].astype(F32)).astype(BF16)
    a2r = send(pa.at[:, xp], ta2.at[0], rss, 3, right)
    a1l.wait_recv()
    pa[1, xm] = (pa[1, xm].astype(F32) + ta1[1].astype(F32)).astype(BF16)
    a2l = send(pa.at[:, xm], ta2.at[1], rss, 4, left)
    b1.wait_recv()
    pb[ys, x2] = (pb[ys, x2].astype(F32) + tb1[x2].astype(F32)).astype(BF16)
    b2r = send(pb.at[ys, x2, pl.ds(0, mid)], tb2.at[0], rss, 5, right)
    b2l = send(pb.at[ys, x2, pl.ds(mid, mid)], tb2.at[1], rss, 6, left)
    for spot in (xp, xm):
        pb[ys, spot] = (pb[ys, spot].astype(F32) + tb1[spot].astype(F32)).astype(BF16)
    a2r.wait_recv()
    a2l.wait_recv()
    for k in range(2):
        sa[k] = (
            pa[k, x].astype(F32) + ta2[0, k].astype(F32) + ta2[1, k].astype(F32)
        ).astype(BF16)
    a3 = send(sa.at[yo], ta3, rss, 7, pair)
    b2r.wait_recv()
    pb[ys, xp, 0:mid] = (pb[ys, xp, 0:mid].astype(F32) + tb2[0].astype(F32)).astype(BF16)
    b3r = send(pb.at[ys, xp], tb3.at[0], rss, 8, right)
    b2l.wait_recv()
    pb[ys, xm, mid:block] = (pb[ys, xm, mid:block].astype(F32) + tb2[1].astype(F32)).astype(BF16)
    b3l = send(pb.at[ys, xm], tb3.at[1], rss, 9, left)
    own_b = pb[ys, x].astype(F32) + tb1[x].astype(F32)
    a3.wait_recv()
    final_a = sa[ys].astype(F32) + ta3[...].astype(F32)
    b3r.wait_recv()
    b3l.wait_recv()
    final_b = own_b + tb3[0].astype(F32) + tb3[1].astype(F32)

    for d in range(nz):
        ret_out[d, :, :half_cols] = final_a[d * cap : (d + 1) * cap].astype(BF16)
        ret_out[d, :, half_cols:] = final_b[d * cap : (d + 1) * cap].astype(BF16)
    home = [
        send(ret_out.at[d], ret_in.at[d - 1], zs, nz - 2 + d, behind(d)) for d in far_first
    ]
    weights = jnp.where(named[0], egates[0], 0.0) + jnp.where(named[1], egates[1], 0.0)
    weights = placing * weights
    high = weights.astype(BF16)
    low = (weights - high.astype(F32)).astype(BF16)
    both = jnp.concatenate([high, low], axis=0)
    for copy in home:
        copy.wait_recv()
    back = jnp.concatenate(
        [ret_out[0].astype(F32)] + [ret_in[d].astype(F32) for d in range(nz - 1)], axis=0
    ).astype(BF16)
    mixed = jnp.dot(both, back, preferred_element_type=F32)
    mix_ref[...] = (mixed[:rows] + mixed[rows:]).astype(BF16)
    for copy in started:
        copy.wait_send()


def layer(
    table, lengths, q, head_route, head_gate, residual, gain, route, egate,
    kv_cache, out_weight, gate_up, down,
):
    pool, _, page, head_width = kv_cache.shape
    experts = out_weight.shape[0]
    tokens = q.shape[1]
    rows, width = residual.shape
    nz = tokens // rows
    half_cols = width // 2
    hidden = down.shape[0]
    cap = max(2, 2 * TOPA * rows // nz)
    block = nz * cap
    amount = 8 * block
    units = 4 * hidden
    vmem = pl.BlockSpec(memory_space=pltpu.VMEM)
    smem = pl.BlockSpec(memory_space=pltpu.SMEM)
    hbm = pl.BlockSpec(memory_space=pl.ANY)

    def buf(*shape):
        return pltpu.VMEM(shape, BF16)

    def dma(n):
        return pltpu.SemaphoreType.DMA((n,))

    return pl.pallas_call(
        layer_kernel,
        out_shape=(
            jax.ShapeDtypeStruct((rows, width), BF16),
            jax.ShapeDtypeStruct((rows, width), BF16),
        ),
        in_specs=[smem] * 2 + [vmem] * 7 + [hbm] * 4,
        out_specs=(vmem, vmem),
        scratch_shapes=[
            buf(pool, 2, page, head_width),
            buf(experts, head_width, width),
            pltpu.VMEM((TOPA, tokens, head_width), F32),
            buf(tokens, experts * head_width),
            buf(nz, rows, width),
            buf(nz - 1, rows, width),
            buf(nz, cap, width),
            buf(nz - 1, cap, width),
            buf(2, 4, block, half_cols),
            buf(2, 4, block, half_cols),
            buf(units, width),
            buf(units, width),
            buf(units, width),
            buf(amount, units),
            buf(2, 4, block, half_cols),
            buf(2, 4, block, half_cols),
            buf(2, block, half_cols),
            buf(2, 2, block, half_cols),
            buf(2, block, half_cols),
            buf(block, half_cols),
            buf(4, block, half_cols),
            buf(2, block // 2, half_cols),
            buf(2, block, half_cols),
            buf(nz, cap, width),
            buf(nz - 1, cap, width),
            dma(1), dma(experts),
            dma(4 * (nz - 1)), dma(4 * (nz - 1)), dma(2 * (nz - 1)), dma(2 * (nz - 1)),
            dma(10), dma(10), dma(10), dma(10), dma(9), dma(9), dma(3),
        ],
        compiler_params=pltpu.CompilerParams(
            collective_id=0, has_side_effects=True, vmem_limit_bytes=VMEM_LIMIT
        ),
        name="layer",
    )(
        table, lengths, q, head_route, head_gate, residual, gain, route, egate,
        kv_cache, out_weight, gate_up, down,
    )


def local(
    residual, queries, kv_cache, page_table, seq_lengths, head_route, head_gate, out_weight,
    norm_gain, expert_route, expert_gate, gate_up, down_weight,
):
    return layer(
        page_table, seq_lengths, jnp.transpose(queries, (1, 0, 2)), head_route.T, head_gate.T,
        residual, norm_gain.reshape(1, -1), expert_route.T, expert_gate.T,
        kv_cache, out_weight, jnp.transpose(gate_up[0], (0, 2, 1)), down_weight[0],
    )


def solution(mesh):
    return jax.shard_map(
        local,
        mesh=mesh,
        in_specs=(
            P(("req", "exp"), None),
            P("req", None, "exp"),
            P("req", None, None, "exp"),
            P("req", None),
            P("req"),
            P("req", None),
            P("req", None),
            P(None, "exp", None),
            P(),
            P(("req", "exp"), None),
            P(("req", "exp"), None),
            P("exp", None, None, "req"),
            P("exp", "req", None),
        ),
        out_specs=(P(("req", "exp"), None), P(("req", "exp"), None)),
        check_vma=False,
    )
```

time: 118 us -> 104 us (0.88)
  Pallas kernels: 105 us -> 98.1 us
  local copies, waits for them, and re-layouts: 11.3 us -> 4.52 us
    pallas_call x2 -> x1, Pallas kernels: 105 us -> 98.1 us  [layer(): pl.pallas_call(layer_kernel, out_shape=(jax.ShapeDtypeStruct((rows, width...]
    unnamed x9 -> x3, local copies, waits for them, and re-layouts: 10 us -> 4.52 us
    squeeze x1 -> x0, local copies, waits for them, and re-layouts: 1.3 us -> none  [local(): turned[1]]
where the time goes in v2:
time: 104 us; the launch traced here: 103 us
  Pallas kernels  98.1 us (94%)
  local copies, waits for them, and re-layouts  4.52 us (4%)
    pallas_call x1, Pallas kernels, layer(): pl.pallas_call(layer_kernel, out_shape=(jax.ShapeDtypeStruct((rows, width...  98.1 us
    unnamed x3, local copies, waits for them, and re-layouts  4.52 us

profile of v2, /device:TPU:2, one launch (start us, length us, event | category | flops | bytes accessed | tf_op | source)
XLA Modules:
  0.0 103.2 jit_solution(17368558406866403303)
XLA Ops:
  0.6 1.6 %copy.17 = bf16[128,2,256]{2,0,1:T(8,128)(2,1)} copy(bf16[128,2,256]{2,1,0:T(2,128)(2,1)} %param.14) | data formatting | bytes 262144 | tf_op args[1]
  2.2 98.1 %layer.1 = (bf16[16,2048]{1,0:T(8,128)(2,1)}, bf16[16,2048]{1,0:T(8,128)(2,1)}) custom-call(s32[9,11]{1,0:T(8,128)} %table.1, s32[9]{0:T(128)} %lengths.1, bf16[2,128,256]{2,1,0:T(8,128)(2,1)} %bitcast.14, s32[2,128]{1,0:T(2,128)} %bitcast.16, f32[2,128]{1,0:T(2,128)} %bitcast.17, bf16[16,2048]{1,0:T(8,128)(2,1)} %residual.1, f32[1,2048]{1,0:T(1,128)} %bitcast.15, ...), custom_call_target="tpu_custom_call" | custom-call | tf_op jit(solution)/shard_map/layer/pallas_call | solution.py:366
  100.3 1.5 %copy.20 = bf16[16,2048]{1,0:T(8,128)(2,1)} copy(bf16[16,2048]{1,0:T(8,128)(2,1)} %get-tuple-element.4) | data formatting | bytes 131072
  101.7 1.5 %copy.21 = bf16[16,2048]{1,0:T(8,128)(2,1)} copy(bf16[16,2048]{1,0:T(8,128)(2,1)} %get-tuple-element.5) | data formatting | bytes 131072

commit v3 on v2

--- a/solution.py
+++ b/solution.py
@@ -223,98 +223,150 @@
     ra[ys, x] = arrived[:, :half_cols]
     rb[ys, x] = arrived[:, half_cols:]
     mid = block // 2
-    a_y = send(ra.at[ys, x], ra.at[ys, x], ags, 0, pair)
-    b_r = send(rb.at[ys, x], rb.at[ys, x], ags, 1, right)
-    b_l = send(rb.at[ys, x], rb.at[ys, x], ags, 2, left)
+    low_rows, high_rows = pl.ds(0, mid), pl.ds(mid, mid)
+
+    def forward(buffer, i, device, *spot):
+        return send(buffer.at[spot], buffer.at[spot], ags, i, device)
+
+    a_y = forward(ra, 0, pair, ys, x)
+    b_r = forward(rb, 1, right, ys, x)
+    b_l = forward(rb, 2, left, ys, x)
+    a_r = forward(ra, 3, right, ys, x)
+    a_l = forward(ra, 4, left, ys, x)
+    b_y = forward(rb, 5, pair, ys, x)
+    w_d = []
+
+    def relay_weights(i):
+        w_y[i].wait_recv()
+        w_d.append(send(part(stores[i], 1), part(stores[i], 3), ws, 6 + i, core))
+
+    relay_weights(0)
+    b_r.wait_recv()
+    b_r2 = forward(rb, 6, right, ys, xm, low_rows)
+    b_ym = forward(rb, 7, pair, ys, xm)
+    b_l.wait_recv()
+    b_l2 = forward(rb, 8, left, ys, xp, high_rows)
+    b_yp = forward(rb, 9, pair, ys, xp)
     a_y.wait_recv()
-    a_r = send(ra.at[:, x], ra.at[:, x], ags, 3, right)
-    a_l = send(ra.at[:, x], ra.at[:, x], ags, 4, left)
-    b_r.wait_recv()
-    b_r2 = send(rb.at[ys, xm, pl.ds(0, mid)], rb.at[ys, xm, pl.ds(0, mid)], ags, 5, right)
-    b_l.wait_recv()
-    b_l2 = send(rb.at[ys, xp, pl.ds(mid, mid)], rb.at[ys, xp, pl.ds(mid, mid)], ags, 6, left)
+    a_or = forward(ra, 10, right, yo, x)
+    a_ol = forward(ra, 11, left, yo, x)
+    relay_weights(1)
+    a_r.wait_recv()
+    a_r2 = forward(ra, 12, right, ys, xm, low_rows)
+    a_l.wait_recv()
+    a_l2 = forward(ra, 13, left, ys, xp, high_rows)
     b_r2.wait_recv()
     b_l2.wait_recv()
-    b_y = send(rb.at[ys], rb.at[ys], ags, 7, pair)
-    a_r.wait_recv()
-    a_r2 = send(ra.at[0, xm], ra.at[0, xm], ags, 8, right)
-    a_l.wait_recv()
-    a_l2 = send(ra.at[1, xp], ra.at[1, xp], ags, 9, left)
-    w_d = []
-    for i in range(2):
-        w_y[i].wait_recv()
-        w_d.append(send(part(stores[i], 1), part(stores[i], 3), ws, 6 + i, core))
-    a_r2.wait_recv()
-    a_l2.wait_recv()
-    b_y.wait_recv()
+    b_y2 = forward(rb, 14, pair, ys, x2)
+
+    units = act.shape[2]
+    step = 256
+
+    def wide(x_half, w_half):
+        return lax.dot_general(
+            x_half, w_half, (((1,), (1,)), ((), ())), preferred_element_type=F32
+        )
+
+    def up_project(spot):
+        xa = ra[:, spot].reshape(2 * block, half_cols)
+        xb = rb[:, spot].reshape(2 * block, half_cols)
+        for n in range(0, units, step):
+            size = min(step, units - n)
+            here = slice(n, n + size)
+            gate_part = wide(xa, wg[here, :half_cols]) + wide(xb, wg[here, half_cols:])
+            up_part = wide(xa, wu[here, :half_cols]) + wide(xb, wu[here, half_cols:])
+            act[spot, :, here] = (
+                gate_part / (1.0 + jnp.exp(-gate_part)) * up_part
+            ).astype(BF16)
+
+    def down_project(spot):
+        for n in range(0, half_cols, 2 * step):
+            for store, base in ((pb, half_cols), (pa, 0)):
+                store[:, spot, :, n : n + 2 * step] = jnp.dot(
+                    act[spot], wd[:, base + n : base + n + 2 * step], preferred_element_type=F32
+                ).astype(BF16).reshape(2, block, 2 * step)
+
     for i in range(2):
         w_c[i].wait_recv()
         w_d[i].wait_recv()
         w_l[i].wait()
-
-    amount = act.shape[0]
-    xa = ra[...].reshape(amount, half_cols)
-    xb = rb[...].reshape(amount, half_cols)
-
-    def wide(x_half, w_half):
-        return lax.dot_general(
-            x_half, w_half, (((1,), (1,)), ((), ())), preferred_element_type=F32
-        )
-
-    units = act.shape[1]
-    step = 256
-    for n in range(0, units, step):
-        size = min(step, units - n)
-        gate_part = wide(xa, wg[n : n + size, :half_cols]) + wide(xb, wg[n : n + size, half_cols:])
-        up_part = wide(xa, wu[n : n + size, :half_cols]) + wide(xb, wu[n : n + size, half_cols:])
-        act[:, n : n + size] = (
-            gate_part / (1.0 + jnp.exp(-gate_part)) * up_part
-        ).astype(BF16)
-    w_y[2].wait_recv()
-    w_d.append(send(part(wd, 1), part(wd, 3), ws, 8, core))
+    b_y.wait_recv()
+    up_project(x)
+    a_or.wait_recv()
+    a_or2 = forward(ra, 15, right, yo, xm, low_rows)
+    a_ol.wait_recv()
+    a_ol2 = forward(ra, 16, left, yo, xp, high_rows)
+    b_ym.wait_recv()
+    up_project(xm)
+    relay_weights(2)
+    b_yp.wait_recv()
+    up_project(xp)
+    for copy in (a_r2, a_l2, a_or2, a_ol2, b_y2):
+        copy.wait_recv()
+    up_project(x2)
     w_c[2].wait_recv()
     w_l[2].wait()
     w_d[2].wait_recv()
-    for n in range(0, half_cols, step):
-        for store, base in ((pa, 0), (pb, half_cols)):
-            store[:, :, :, n : n + step] = jnp.dot(
-                act[...], wd[:, base + n : base + n + step], preferred_element_type=F32
-            ).astype(BF16).reshape(2, 4, block, step)
-
-    b1 = send(pb.at[yo], tb1, rss, 0, pair)
-    a1r = send(pa.at[0, x2], ta1.at[0], rss, 1, right)
-    a1l = send(pa.at[1, x2], ta1.at[1], rss, 2, left)
+
+    down_project(x2)
+    a1r = send(pa.at[yo, x2, low_rows], ta1.at[0, 0], rss, 0, right)
+    a1l = send(pa.at[yo, x2, high_rows], ta1.at[0, 1], rss, 1, left)
+    b1_2 = send(pb.at[yo, x2], tb1.at[0], rss, 2, pair)
+    a1rs = send(pa.at[ys, x2, low_rows], ta1.at[1, 0], rss, 3, right)
+    a1ls = send(pa.at[ys, x2, high_rows], ta1.at[1, 1], rss, 4, left)
+    down_project(xp)
+    b1_p = send(pb.at[yo, xp], tb1.at[1], rss, 5, pair)
+    down_project(xm)
+    b1_m = send(pb.at[yo, xm], tb1.at[2], rss, 6, pair)
+
+    def add(store, term, *spot):
+        store[spot] = (store[spot].astype(F32) + term.astype(F32)).astype(BF16)
+
+    low, high = slice(0, mid), slice(mid, block)
     a1r.wait_recv()
-    pa[0, xp] = (pa[0, xp].astype(F32) + ta1[0].astype(F32)).astype(BF16)
-    a2r = send(pa.at[:, xp], ta2.at[0], rss, 3, right)
+    add(pa, ta1[0, 0], yo, xp, low)
+    a2r = send(pa.at[yo, xp], ta2.at[0, 0], rss, 7, right)
     a1l.wait_recv()
-    pa[1, xm] = (pa[1, xm].astype(F32) + ta1[1].astype(F32)).astype(BF16)
-    a2l = send(pa.at[:, xm], ta2.at[1], rss, 4, left)
-    b1.wait_recv()
-    pb[ys, x2] = (pb[ys, x2].astype(F32) + tb1[x2].astype(F32)).astype(BF16)
-    b2r = send(pb.at[ys, x2, pl.ds(0, mid)], tb2.at[0], rss, 5, right)
-    b2l = send(pb.at[ys, x2, pl.ds(mid, mid)], tb2.at[1], rss, 6, left)
-    for spot in (xp, xm):
-        pb[ys, spot] = (pb[ys, spot].astype(F32) + tb1[spot].astype(F32)).astype(BF16)
+    add(pa, ta1[0, 1], yo, xm, high)
+    a2l = send(pa.at[yo, xm], ta2.at[0, 1], rss, 8, left)
+    b1_2.wait_recv()
+    add(pb, tb1[0], ys, x2)
+    b2r = send(pb.at[ys, x2, low_rows], tb2.at[0], rss, 9, right)
+    b2l = send(pb.at[ys, x2, high_rows], tb2.at[1], rss, 10, left)
+    a1rs.wait_recv()
+    add(pa, ta1[1, 0], ys, xp, low)
+    a2rs = send(pa.at[ys, xp], ta2.at[1, 0], rss, 11, right)
+    a1ls.wait_recv()
+    add(pa, ta1[1, 1], ys, xm, high)
+    a2ls = send(pa.at[ys, xm], ta2.at[1, 1], rss, 12, left)
+    down_project(x)
     a2r.wait_recv()
     a2l.wait_recv()
-    for k in range(2):
-        sa[k] = (
-            pa[k, x].astype(F32) + ta2[0, k].astype(F32) + ta2[1, k].astype(F32)
-        ).astype(BF16)
-    a3 = send(sa.at[yo], ta3, rss, 7, pair)
+    sa[...] = (
+        pa[yo, x].astype(F32) + ta2[0, 0].astype(F32) + ta2[0, 1].astype(F32)
+    ).astype(BF16)
+    a3 = send(sa, ta3, rss, 13, pair)
+    b1_x = send(pb.at[yo, x], tb1.at[3], rss, 14, pair)
+    b1_p.wait_recv()
+    add(pb, tb1[1], ys, xp)
+    b1_m.wait_recv()
+    add(pb, tb1[2], ys, xm)
     b2r.wait_recv()
-    pb[ys, xp, 0:mid] = (pb[ys, xp, 0:mid].astype(F32) + tb2[0].astype(F32)).astype(BF16)
-    b3r = send(pb.at[ys, xp], tb3.at[0], rss, 8, right)
+    add(pb, tb2[0], ys, xp, low)
+    b3r = send(pb.at[ys, xp], tb3.at[0], rss, 15, right)
     b2l.wait_recv()
-    pb[ys, xm, mid:block] = (pb[ys, xm, mid:block].astype(F32) + tb2[1].astype(F32)).astype(BF16)
-    b3l = send(pb.at[ys, xm], tb3.at[1], rss, 9, left)
-    own_b = pb[ys, x].astype(F32) + tb1[x].astype(F32)
+    add(pb, tb2[1], ys, xm, high)
+    b3l = send(pb.at[ys, xm], tb3.at[1], rss, 16, left)
+    a2rs.wait_recv()
+    a2ls.wait_recv()
+    final_a = pa[ys, x].astype(F32) + ta2[1, 0].astype(F32) + ta2[1, 1].astype(F32)
     a3.wait_recv()
-    final_a = sa[ys].astype(F32) + ta3[...].astype(F32)
+    final_a = final_a + ta3[...].astype(F32)
+    b1_x.wait_recv()
+    final_b = pb[ys, x].astype(F32) + tb1[3].astype(F32)
     b3r.wait_recv()
     b3l.wait_recv()
-    final_b = own_b + tb3[0].astype(F32) + tb3[1].astype(F32)
+    final_b = final_b + tb3[0].astype(F32) + tb3[1].astype(F32)
 
     for d in range(nz):
         ret_out[d, :, :half_cols] = final_a[d * cap : (d + 1) * cap].astype(BF16)
@@ -324,9 +376,9 @@
     ]
     weights = jnp.where(named[0], egates[0], 0.0) + jnp.where(named[1], egates[1], 0.0)
     weights = placing * weights
-    high = weights.astype(BF16)
-    low = (weights - high.astype(F32)).astype(BF16)
-    both = jnp.concatenate([high, low], axis=0)
+    coarse = weights.astype(BF16)
+    fine = (weights - coarse.astype(F32)).astype(BF16)
+    both = jnp.concatenate([coarse, fine], axis=0)
     for copy in home:
         copy.wait_recv()
     back = jnp.concatenate(
@@ -351,7 +403,6 @@
     hidden = down.shape[0]
     cap = max(2, 2 * TOPA * rows // nz)
     block = nz * cap
-    amount = 8 * block
     units = 4 * hidden
     vmem = pl.BlockSpec(memory_space=pltpu.VMEM)
     smem = pl.BlockSpec(memory_space=pltpu.SMEM)
@@ -385,12 +436,12 @@
             buf(units, width),
             buf(units, width),
             buf(units, width),
-            buf(amount, units),
+            buf(4, 2 * block, units),
             buf(2, 4, block, half_cols),
             buf(2, 4, block, half_cols),
-            buf(2, block, half_cols),
+            buf(2, 2, block // 2, half_cols),
             buf(2, 2, block, half_cols),
-            buf(2, block, half_cols),
+            buf(block, half_cols),
             buf(block, half_cols),
             buf(4, block, half_cols),
             buf(2, block // 2, half_cols),
@@ -399,7 +450,7 @@
             buf(nz - 1, cap, width),
             dma(1), dma(experts),
             dma(4 * (nz - 1)), dma(4 * (nz - 1)), dma(2 * (nz - 1)), dma(2 * (nz - 1)),
-            dma(10), dma(10), dma(10), dma(10), dma(9), dma(9), dma(3),
+            dma(17), dma(17), dma(17), dma(17), dma(9), dma(9), dma(3),
         ],
         compiler_params=pltpu.CompilerParams(
             collective_id=0, has_side_effects=True, vmem_limit_bytes=VMEM_LIMIT

time: 104 us -> 91.9 us (0.88)
  Pallas kernels: 98.1 us -> 86.2 us
    pallas_call x1, Pallas kernels: 98.1 us -> 86.2 us  [layer(): pl.pallas_call(layer_kernel, out_shape=(jax.ShapeDtypeStruct((rows, width...]
where the time goes in v3:
time: 91.9 us; the launch traced here: 91.3 us
  Pallas kernels  86.2 us (94%)
  local copies, waits for them, and re-layouts  4.52 us (5%)
    pallas_call x1, Pallas kernels, layer(): pl.pallas_call(layer_kernel, out_shape=(jax.ShapeDtypeStruct((rows, width...  86.2 us
    unnamed x3, local copies, waits for them, and re-layouts  4.52 us

profile of v3, /device:TPU:2, one launch (start us, length us, event | category | flops | bytes accessed | tf_op | source)
XLA Modules:
  0.0 91.3 jit_solution(16622935525237591784)
XLA Ops:
  0.6 1.6 %copy.17 = bf16[128,2,256]{2,0,1:T(8,128)(2,1)} copy(bf16[128,2,256]{2,1,0:T(2,128)(2,1)} %param.14) | data formatting | bytes 262144 | tf_op args[1]
  2.2 86.2 %layer.1 = (bf16[16,2048]{1,0:T(8,128)(2,1)}, bf16[16,2048]{1,0:T(8,128)(2,1)}) custom-call(s32[9,11]{1,0:T(8,128)} %table.1, s32[9]{0:T(128)} %lengths.1, bf16[2,128,256]{2,1,0:T(8,128)(2,1)} %bitcast.14, s32[2,128]{1,0:T(2,128)} %bitcast.16, f32[2,128]{1,0:T(2,128)} %bitcast.17, bf16[16,2048]{1,0:T(8,128)(2,1)} %residual.1, f32[1,2048]{1,0:T(1,128)} %bitcast.15, ...), custom_call_target="tpu_custom_call" | custom-call | tf_op jit(solution)/shard_map/layer/pallas_call | solution.py:417
  88.4 1.5 %copy.20 = bf16[16,2048]{1,0:T(8,128)(2,1)} copy(bf16[16,2048]{1,0:T(8,128)(2,1)} %get-tuple-element.4) | data formatting | bytes 131072
  89.9 1.5 %copy.21 = bf16[16,2048]{1,0:T(8,128)(2,1)} copy(bf16[16,2048]{1,0:T(8,128)(2,1)} %get-tuple-element.5) | data formatting | bytes 131072

commit v4 on v3

--- a/solution.py
+++ b/solution.py
@@ -33,7 +33,7 @@
 def layer_kernel(
     table, lengths, q_ref, head_route, head_gate, residual, gain, route, egate,
     kv_hbm, w_hbm, gu_hbm, d_hbm, attended_ref, mix_ref,
-    kv, w, mix, x_rows, partial, rs_buf, out_buf, in_buf, ra, rb, wg, wu, wd, act, pa, pb,
+    qs, kv, w, mix, x_rows, partial, half_buf, rs_buf, out_buf, in_buf, ra, rb, wg, wu, wd, act, pa, pb,
     ta1, ta2, sa, ta3, tb1, tb2, tb3, ret_out, ret_in,
     kv_sem, o_sem, s_send, s_recv, z_send, z_recv, ag_send, ag_recv, rs_send, rs_recv,
     w_send, w_recv, l_sem,
@@ -80,41 +80,11 @@
     o_copies = [pltpu.make_async_copy(w_hbm.at[e], w.at[e], o_sem.at[e]) for e in range(experts)]
     for copy in o_copies:
         copy.start()
-    pl.semaphore_wait(barrier, len(others))
-
-    started = []
-
-    def send(src, dst, sems, i, device):
-        copy = pltpu.make_async_remote_copy(
-            src_ref=src, dst_ref=dst, send_sem=sems[0].at[i], recv_sem=sems[1].at[i],
-            device_id=device, device_id_type=MESH,
-        )
-        copy.start()
-        started.append(copy)
-        return copy
-
-    zs, ags, rss, ws = (z_send, z_recv), (ag_send, ag_recv), (rs_send, rs_recv), (w_send, w_recv)
-    ss = (s_send, s_recv)
-    far_first = (4, 3, 5, 2, 6, 1, 7)
-
-    sources, stores = (gu_hbm.at[0], gu_hbm.at[1], d_hbm), (wg, wu, wd)
-
-    def part(store, b):
-        return store.at[pl.ds(b * hidden, hidden)]
-
-    w_y = [send(sources[i], part(stores[i], 1), ws, i, w_pair) for i in range(3)]
-    w_c = [send(sources[i], part(stores[i], 2), ws, 3 + i, core) for i in range(3)]
-    w_l = [
-        pltpu.make_async_copy(sources[i], part(stores[i], 0), l_sem.at[i]) for i in range(3)
-    ]
-    for copy in w_l:
-        copy.start()
-
     pages = table.shape[1]
     decodes = table.shape[0] - 1
     page = kv.shape[2]
     width = q_ref.shape[2]
-    tokens = q_ref.shape[1]
+    tokens = q_ref.shape[0]
     keys = pages * page
     row_pos = lengths[0] - SPAN + lax.broadcasted_iota(jnp.int32, (tokens, keys), 0)
     causal = lax.broadcasted_iota(jnp.int32, (tokens, keys), 1) <= row_pos
@@ -127,6 +97,43 @@
     for s in range(decodes):
         length_of = jnp.where(d_slot == s, lengths[s + 1], length_of)
     d_allowed = (d_slot == d_row) & (d_col % page < length_of)
+    pl.semaphore_wait(barrier, len(others))
+
+    started = []
+
+    def send(src, dst, sems, i, device):
+        copy = pltpu.make_async_remote_copy(
+            src_ref=src, dst_ref=dst, send_sem=sems[0].at[i], recv_sem=sems[1].at[i],
+            device_id=device, device_id_type=MESH,
+        )
+        copy.start()
+        started.append(copy)
+        return copy
+
+    zs, ags, rss, ws = (z_send, z_recv), (ag_send, ag_recv), (rs_send, rs_recv), (w_send, w_recv)
+    ss = (s_send, s_recv)
+    far_first = (4, 3, 5, 2, 6, 1, 7)
+
+    a_cols, b_cols, all_cols = pl.ds(0, half_cols), pl.ds(half_cols, half_cols), slice(None)
+    parts = (
+        (gu_hbm.at[0], wg, all_cols), (gu_hbm.at[1], wu, all_cols),
+        (d_hbm, wd, b_cols), (d_hbm, wd, a_cols),
+    )
+
+    def source(i):
+        return parts[i][0].at[:, parts[i][2]]
+
+    def part(i, b):
+        return parts[i][1].at[pl.ds(b * hidden, hidden), parts[i][2]]
+
+    w_y = [send(source(i), part(i, 1), ws, i, w_pair) for i in range(4)]
+    w_c = [send(source(i), part(i, 2), ws, 4 + i, core) for i in range(4)]
+    w_l = [pltpu.make_async_copy(source(i), part(i, 0), l_sem.at[i]) for i in range(4)]
+    for copy in w_l:
+        copy.start()
+
+    for t in range(TOPA):
+        qs[t] = q_ref[:, t, :]
     kv_copy.wait()
     for h in range(width // HD):
         cols = slice(h * HD, (h + 1) * HD)
@@ -137,11 +144,11 @@
         pre = [(0, p) for p in range(pages)]
         k_pre, v_pre = paged(0, pre), paged(1, pre)
         for t in range(TOPA):
-            mix[t, :, cols] = attend(q_ref[t, :, cols], k_pre, v_pre, causal)
+            mix[t, :, cols] = attend(qs[t, :, cols], k_pre, v_pre, causal)
         dec = [(s + 1, 0) for s in range(decodes)]
         k_dec, v_dec = paged(0, dec), paged(1, dec)
         q_dec = jnp.concatenate(
-            [q_ref[t, tokens - tail : tokens, cols] for t in range(TOPA)], axis=0
+            [qs[t, tokens - tail : tokens, cols] for t in range(TOPA)], axis=0
         )
         o_dec = attend(q_dec, k_dec, v_dec, d_allowed)
         for t in range(TOPA):
@@ -159,21 +166,49 @@
 
     outs = w.shape[2]
     chunk = outs // 4
-    scatter = []
-    for n in range(0, outs, chunk):
-        partial[:, :, n : n + chunk] = jnp.dot(
+    scatter, halves = [], []
+
+    def block_cols(k, part_of):
+        return pl.ds(k * chunk + part_of * (chunk // 2), chunk // 2)
+
+    def scatter_send(k, d):
+        cols = pl.ds(k * chunk, chunk)
+        scatter.append(
+            send(
+                partial.at[lax.rem(z + d, nz), :, cols], rs_buf.at[d - 1, :, cols],
+                ss, k * nz + d - 1, ahead(d),
+            )
+        )
+
+    def pass_on(k):
+        for side, d in ((0, nz // 2 - 1), (1, nz // 2 + 1)):
+            halves[2 * k + side].wait_recv()
+            spot, cols = lax.rem(z + d, nz), block_cols(k, side)
+            partial[spot, :, cols] = (
+                partial[spot, :, cols].astype(F32) + half_buf[side, :, cols].astype(F32)
+            ).astype(BF16)
+            scatter_send(k, d)
+
+    for k in range(outs // chunk):
+        partial[:, :, k * chunk : (k + 1) * chunk] = jnp.dot(
             x_rows[...],
-            w[:, :, n : n + chunk].reshape(experts * width, chunk),
+            w[:, :, k * chunk : (k + 1) * chunk].reshape(experts * width, chunk),
             preferred_element_type=F32,
         ).astype(BF16).reshape(nz, rows, chunk)
-        for d in far_first:
-            scatter.append(
+        far = lax.rem(z + nz // 2, nz)
+        for side, device in ((0, ahead(1)), (1, behind(1))):
+            cols = block_cols(k, side)
+            halves.append(
                 send(
-                    partial.at[lax.rem(z + d, nz), :, pl.ds(n, chunk)],
-                    rs_buf.at[d - 1, :, pl.ds(n, chunk)],
-                    ss, (n // chunk) * (nz - 1) + d - 1, ahead(d),
+                    partial.at[far, :, cols], half_buf.at[side, :, cols],
+                    ss, k * nz + (nz // 2 - 1 if side == 0 else nz - 1), device,
                 )
             )
+        for d in (2, 6, 1, 7):
+            scatter_send(k, d)
+        if k > 0:
+            pass_on(k - 1)
+    pass_on(outs // chunk - 1)
 
     def routed(t):
         rel = column(route[t : t + 1].astype(F32)) - z.astype(F32)
@@ -196,8 +231,9 @@
     for copy in scatter:
         copy.wait_recv()
     summed = residual[...].astype(F32) + partial[z].astype(F32)
-    for d in range(nz - 1):
-        summed = summed + rs_buf[d].astype(F32)
+    for d in range(1, nz):
+        if d != nz // 2:
+            summed = summed + rs_buf[d - 1].astype(F32)
     attended = summed.astype(BF16)
     attended_ref[...] = attended
     values = attended.astype(F32)
@@ -238,7 +274,12 @@
 
     def relay_weights(i):
         w_y[i].wait_recv()
-        w_d.append(send(part(stores[i], 1), part(stores[i], 3), ws, 6 + i, core))
+        w_d.append(send(part(i, 1), part(i, 3), ws, 8 + i, core))
+
+    def have_weights(i):
+        w_c[i].wait_recv()
+        w_d[i].wait_recv()
+        w_l[i].wait()
 
     relay_weights(0)
     b_r.wait_recv()
@@ -279,17 +320,14 @@
                 gate_part / (1.0 + jnp.exp(-gate_part)) * up_part
             ).astype(BF16)
 
-    def down_project(spot):
+    def down_project(store, base, spot):
         for n in range(0, half_cols, 2 * step):
-            for store, base in ((pb, half_cols), (pa, 0)):
-                store[:, spot, :, n : n + 2 * step] = jnp.dot(
-                    act[spot], wd[:, base + n : base + n + 2 * step], preferred_element_type=F32
-                ).astype(BF16).reshape(2, block, 2 * step)
-
-    for i in range(2):
-        w_c[i].wait_recv()
-        w_d[i].wait_recv()
-        w_l[i].wait()
+            store[:, spot, :, n : n + 2 * step] = jnp.dot(
+                act[spot], wd[:, base + n : base + n + 2 * step], preferred_element_type=F32
+            ).astype(BF16).reshape(2, block, 2 * step)
+
+    have_weights(0)
+    have_weights(1)
     b_y.wait_recv()
     up_project(x)
     a_or.wait_recv()
@@ -304,65 +342,65 @@
     for copy in (a_r2, a_l2, a_or2, a_ol2, b_y2):
         copy.wait_recv()
     up_project(x2)
-    w_c[2].wait_recv()
-    w_l[2].wait()
-    w_d[2].wait_recv()
-
-    down_project(x2)
-    a1r = send(pa.at[yo, x2, low_rows], ta1.at[0, 0], rss, 0, right)
-    a1l = send(pa.at[yo, x2, high_rows], ta1.at[0, 1], rss, 1, left)
-    b1_2 = send(pb.at[yo, x2], tb1.at[0], rss, 2, pair)
-    a1rs = send(pa.at[ys, x2, low_rows], ta1.at[1, 0], rss, 3, right)
-    a1ls = send(pa.at[ys, x2, high_rows], ta1.at[1, 1], rss, 4, left)
-    down_project(xp)
-    b1_p = send(pb.at[yo, xp], tb1.at[1], rss, 5, pair)
-    down_project(xm)
-    b1_m = send(pb.at[yo, xm], tb1.at[2], rss, 6, pair)
+
+    have_weights(2)
+    b1 = []
+    for n, spot in enumerate((x2, xp, xm, x)):
+        down_project(pb, half_cols, spot)
+        b1.append(send(pb.at[yo, spot], tb1.at[n], rss, n, pair))
 
     def add(store, term, *spot):
         store[spot] = (store[spot].astype(F32) + term.astype(F32)).astype(BF16)
 
     low, high = slice(0, mid), slice(mid, block)
+    relay_weights(3)
+    b1[0].wait_recv()
+    add(pb, tb1[0], ys, x2)
+    b2r = send(pb.at[ys, x2, low_rows], tb2.at[0], rss, 4, right)
+    b2l = send(pb.at[ys, x2, high_rows], tb2.at[1], rss, 5, left)
+    have_weights(3)
+    down_project(pa, 0, x2)
+    a1r = send(pa.at[yo, x2, low_rows], ta1.at[0, 0], rss, 6, right)
+    a1l = send(pa.at[yo, x2, high_rows], ta1.at[0, 1], rss, 7, left)
+    a1rs = send(pa.at[ys, x2, low_rows], ta1.at[1, 0], rss, 8, right)
+    a1ls = send(pa.at[ys, x2, high_rows], ta1.at[1, 1], rss, 9, left)
+    down_project(pa, 0, xp)
+    down_project(pa, 0, xm)
     a1r.wait_recv()
     add(pa, ta1[0, 0], yo, xp, low)
-    a2r = send(pa.at[yo, xp], ta2.at[0, 0], rss, 7, right)
+    a2r = send(pa.at[yo, xp], ta2.at[0, 0], rss, 10, right)
     a1l.wait_recv()
     add(pa, ta1[0, 1], yo, xm, high)
-    a2l = send(pa.at[yo, xm], ta2.at[0, 1], rss, 8, left)
-    b1_2.wait_recv()
-    add(pb, tb1[0], ys, x2)
-    b2r = send(pb.at[ys, x2, low_rows], tb2.at[0], rss, 9, right)
-    b2l = send(pb.at[ys, x2, high_rows], tb2.at[1], rss, 10, left)
+    a2l = send(pa.at[yo, xm], ta2.at[0, 1], rss, 11, left)
     a1rs.wait_recv()
     add(pa, ta1[1, 0], ys, xp, low)
-    a2rs = send(pa.at[ys, xp], ta2.at[1, 0], rss, 11, right)
+    a2rs = send(pa.at[ys, xp], ta2.at[1, 0], rss, 12, right)
     a1ls.wait_recv()
     add(pa, ta1[1, 1], ys, xm, high)
-    a2ls = send(pa.at[ys, xm], ta2.at[1, 1], rss, 12, left)
-    down_project(x)
+    a2ls = send(pa.at[ys, xm], ta2.at[1, 1], rss, 13, left)
+    b1[1].wait_recv()
+    add(pb, tb1[1], ys, xp)
+    b1[2].wait_recv()
+    add(pb, tb1[2], ys, xm)
+    b2r.wait_recv()
+    add(pb, tb2[0], ys, xp, low)
+    b3r = send(pb.at[ys, xp], tb3.at[0], rss, 14, right)
+    b2l.wait_recv()
+    add(pb, tb2[1], ys, xm, high)
+    b3l = send(pb.at[ys, xm], tb3.at[1], rss, 15, left)
+    down_project(pa, 0, x)
     a2r.wait_recv()
     a2l.wait_recv()
     sa[...] = (
         pa[yo, x].astype(F32) + ta2[0, 0].astype(F32) + ta2[0, 1].astype(F32)
     ).astype(BF16)
-    a3 = send(sa, ta3, rss, 13, pair)
-    b1_x = send(pb.at[yo, x], tb1.at[3], rss, 14, pair)
-    b1_p.wait_recv()
-    add(pb, tb1[1], ys, xp)
-    b1_m.wait_recv()
-    add(pb, tb1[2], ys, xm)
-    b2r.wait_recv()
-    add(pb, tb2[0], ys, xp, low)
-    b3r = send(pb.at[ys, xp], tb3.at[0], rss, 15, right)
-    b2l.wait_recv()
-    add(pb, tb2[1], ys, xm, high)
-    b3l = send(pb.at[ys, xm], tb3.at[1], rss, 16, left)
+    a3 = send(sa, ta3, rss, 16, pair)
     a2rs.wait_recv()
     a2ls.wait_recv()
     final_a = pa[ys, x].astype(F32) + ta2[1, 0].astype(F32) + ta2[1, 1].astype(F32)
     a3.wait_recv()
     final_a = final_a + ta3[...].astype(F32)
-    b1_x.wait_recv()
+    b1[3].wait_recv()
     final_b = pb[ys, x].astype(F32) + tb1[3].astype(F32)
     b3r.wait_recv()
     b3l.wait_recv()
@@ -396,7 +434,7 @@
 ):
     pool, _, page, head_width = kv_cache.shape
     experts = out_weight.shape[0]
-    tokens = q.shape[1]
+    tokens = q.shape[0]
     rows, width = residual.shape
     nz = tokens // rows
     half_cols = width // 2
@@ -423,11 +461,13 @@
         in_specs=[smem] * 2 + [vmem] * 7 + [hbm] * 4,
         out_specs=(vmem, vmem),
         scratch_shapes=[
+            buf(TOPA, tokens, head_width),
             buf(pool, 2, page, head_width),
             buf(experts, head_width, width),
             pltpu.VMEM((TOPA, tokens, head_width), F32),
             buf(tokens, experts * head_width),
             buf(nz, rows, width),
+            buf(2, rows, width),
             buf(nz - 1, rows, width),
             buf(nz, cap, width),
             buf(nz - 1, cap, width),
@@ -449,8 +489,8 @@
             buf(nz, cap, width),
             buf(nz - 1, cap, width),
             dma(1), dma(experts),
-            dma(4 * (nz - 1)), dma(4 * (nz - 1)), dma(2 * (nz - 1)), dma(2 * (nz - 1)),
-            dma(17), dma(17), dma(17), dma(17), dma(9), dma(9), dma(3),
+            dma(4 * nz), dma(4 * nz), dma(2 * (nz - 1)), dma(2 * (nz - 1)),
+            dma(17), dma(17), dma(17), dma(17), dma(12), dma(12), dma(4),
         ],
         compiler_params=pltpu.CompilerParams(
             collective_id=0, has_side_effects=True, vmem_limit_bytes=VMEM_LIMIT
@@ -467,7 +507,7 @@
     norm_gain, expert_route, expert_gate, gate_up, down_weight,
 ):
     return layer(
-        page_table, seq_lengths, jnp.transpose(queries, (1, 0, 2)), head_route.T, head_gate.T,
+        page_table, seq_lengths, queries, head_route.T, head_gate.T,
         residual, norm_gain.reshape(1, -1), expert_route.T, expert_gate.T,
         kv_cache, out_weight, jnp.transpose(gate_up[0], (0, 2, 1)), down_weight[0],
     )

time: 91.9 us -> 88.6 us (0.964)
  Pallas kernels: 86.2 us -> 84.4 us
  local copies, waits for them, and re-layouts: 4.52 us -> 2.95 us
    pallas_call x1, Pallas kernels: 86.2 us -> 84.4 us  [layer(): pl.pallas_call(layer_kernel, out_shape=(jax.ShapeDtypeStruct((rows, width...]
    unnamed x3 -> x2, local copies, waits for them, and re-layouts: 4.52 us -> 2.95 us
where the time goes in v4:
time: 88.6 us; the launch traced here: 88 us
  Pallas kernels  84.4 us (95%)
  local copies, waits for them, and re-layouts  2.95 us (3%)
    pallas_call x1, Pallas kernels, layer(): pl.pallas_call(layer_kernel, out_shape=(jax.ShapeDtypeStruct((rows, width...  84.4 us
    unnamed x2, local copies, waits for them, and re-layouts  2.95 us

profile of v4, /device:TPU:2, one launch (start us, length us, event | category | flops | bytes accessed | tf_op | source)
XLA Modules:
  0.0 88.0 jit_solution(1387082745133609439)
XLA Ops:
  0.6 84.4 %layer.1 = (bf16[16,2048]{1,0:T(8,128)(2,1)}, bf16[16,2048]{1,0:T(8,128)(2,1)}) custom-call(s32[9,11]{1,0:T(8,128)} %table.1, s32[9]{0:T(128)} %lengths.1, bf16[128,2,256]{2,1,0:T(2,128)(2,1)} %q_ref.1, s32[2,128]{1,0:T(2,128)} %bitcast.12, f32[2,128]{1,0:T(2,128)} %bitcast.13, bf16[16,2048]{1,0:T(8,128)(2,1)} %residual.1, f32[1,2048]{1,0:T(1,128)} %bitcast.11, ...), custom_call_target="tpu_custom_call" | custom-call | tf_op jit(solution)/shard_map/layer/pallas_call | solution.py:455
  85.0 1.5 %copy.17 = bf16[16,2048]{1,0:T(8,128)(2,1)} copy(bf16[16,2048]{1,0:T(8,128)(2,1)} %get-tuple-element.4) | data formatting | bytes 131072
  86.5 1.5 %copy.18 = bf16[16,2048]{1,0:T(8,128)(2,1)} copy(bf16[16,2048]{1,0:T(8,128)(2,1)} %get-tuple-element.5) | data formatting | bytes 131072
